TPU v7x, 32 devices: a whole 2x2x4 slice. The times are simulated.
32 devices in a mesh: dp: 4 (over z), heads: 4 (over x, core), tensor: 2 (over y).
Axes of the slice: x: 2, y: 2, z: 4, core: 2. Of those that a mesh axis runs over, the one named last changes fastest.
Arguments:
- inputs: bfloat16 [6304, 768], P(('dp', 'heads', 'tensor')), may hold values from -6 to 6
- first_gain: bfloat16 [768], replicated, may hold values from 0.099609375 to 1.8984375
- first_bias: bfloat16 [768], replicated, may hold values from -2.5 to 2.5
- head_weight: bfloat16 [3, 768, 768], P(None, ('dp', 'tensor'), 'heads'), may hold values from -0.21875 to 0.21875
- head_bias: bfloat16 [2, 768], P(None, ('heads', 'dp', 'tensor')), may hold values from -2.5 to 2.5
- merge_weight: bfloat16 [768, 768], P('heads', ('dp', 'tensor')), may hold values from -0.625 to 0.625
- merge_bias: bfloat16 [768], replicated, may hold values from -2.5 to 2.5
- second_gain: bfloat16 [768], replicated, may hold values from 0.099609375 to 1.8984375
- second_bias: bfloat16 [768], replicated, may hold values from -2.5 to 2.5
- router: bfloat16 [768, 4], replicated, may hold values from -0.15625 to 0.15625
- router_noise: float32 [6304, 4], P(('dp', 'heads', 'tensor')), may hold values from -4 to 4
- expert_ids: int32 [6304, 2], P(('dp', 'heads', 'tensor')), may hold values from 0 to 3, all different within a row; in each aligned block of 197 rows (0 to 196, 197 to 393, ...) at most 128 rows name the same one
- expert_in: bfloat16 [4, 768, 3072], P(None, ('dp', 'heads'), 'tensor'), may hold values from -0.21875 to 0.21875
- expert_in_bias: bfloat16 [4, 3072], P(None, ('tensor', 'dp', 'heads')), may hold values from -2.5 to 2.5
- expert_out: bfloat16 [4, 3072, 768], P(None, 'tensor', ('dp', 'heads')), may hold values from -0.3125 to 0.3125
- expert_out_bias: bfloat16 [4, 768], replicated, may hold values from -2.5 to 2.5
- cotangent: bfloat16 [6304, 768], P(('dp', 'heads', 'tensor')), may hold values from -6 to 6
Outputs:
- output: float32 [6304, 768], P(('dp', 'heads', 'tensor'))
- balance_loss: float32 [], replicated
- input_grad: float32 [6304, 768], P(('dp', 'heads', 'tensor'))
- first_gain_grad: float32 [768], replicated
- first_bias_grad: float32 [768], replicated
- head_weight_grad: float32 [3, 768, 768], P(None, ('dp', 'tensor'), 'heads')
- head_bias_grad: float32 [2, 768], P(None, ('heads', 'dp', 'tensor'))
- merge_weight_grad: float32 [768, 768], P('heads', ('dp', 'tensor'))
- merge_bias_grad: float32 [768], replicated
- second_gain_grad: float32 [768], replicated
- second_bias_grad: float32 [768], replicated
- router_grad: float32 [768, 4], replicated
- expert_in_grad: float32 [4, 768, 3072], P(None, ('dp', 'heads'), 'tensor')
- expert_in_bias_grad: float32 [4, 3072], P(None, ('tensor', 'dp', 'heads'))
- expert_out_grad: float32 [4, 3072, 768], P(None, 'tensor', ('dp', 'heads'))
- expert_out_bias_grad: float32 [4, 768], replicated
Inputs may be any that keep to these rules, and one draw needn't show every extreme that they name: `expert_ids`: each row names two different experts; in the rows of one device no expert is named by more than 128 rows, and in some device's rows an expert is named by exactly 128 rows.
All inputs are finite; a program needn't handle non-finite values.
Results may differ from a plain program's by a relative error of at most 0.025.
Values may be sent and summed in bfloat16 or wider, within the bound.
A program may use at most 192 MiB of HBM per device.

v0:
```python
import jax
import jax.numpy as jnp
from jax import lax
from jax.sharding import PartitionSpec as P

HEAD_DIM = 64
SEQ = 197
CAP = 128


def layer_norm(values, factor, offset):
    average = jnp.mean(values, axis=-1, keepdims=True)
    centred = values - average
    spread = jnp.mean(centred * centred, axis=-1, keepdims=True)
    return centred * lax.rsqrt(spread + 1e-06) * factor + offset


def expert_weights(expert_in, expert_out, expert_in_bias):
    return (
        lax.all_gather(expert_in, ("dp", "heads"), axis=1, tiled=True),
        lax.all_gather(expert_out, ("dp", "heads"), axis=2, tiled=True),
        lax.all_gather(expert_in_bias, ("dp", "heads"), axis=1, tiled=True),
    )


def body(
    inputs,
    first_gain,
    first_bias,
    head_weight,
    head_bias,
    merge_weight,
    merge_bias,
    second_gain,
    second_bias,
    router,
    router_noise,
    expert_ids,
    expert_in,
    expert_in_bias,
    expert_out,
    expert_out_bias,
    cotangent,
):
    tok_rows = inputs.shape[0]
    features = inputs.shape[1]
    experts = expert_in.shape[0]
    head_cols = head_weight.shape[2]
    heads_local = head_cols // HEAD_DIM
    total_tokens = tok_rows * lax.axis_size(("dp", "heads", "tensor"))
    scale = HEAD_DIM ** (-0.5)
    whole_head, whole_merge, whole_bias = (
        lax.all_gather(head_weight, ("dp", "tensor"), axis=1, tiled=True),
        lax.all_gather(merge_weight, ("dp", "tensor"), axis=1, tiled=True),
        lax.all_gather(head_bias, ("dp", "tensor"), axis=1, tiled=True),
    )
    residual_in = inputs.astype(jnp.float32)
    normed, norm_back = jax.vjp(
        layer_norm, residual_in, first_gain.astype(jnp.float32), first_bias.astype(jnp.float32)
    )
    group_rows = lax.all_gather(normed.astype(jnp.bfloat16), "heads", axis=0, tiled=True)
    group_count = group_rows.shape[0]
    group_images = group_count // SEQ
    projected = jnp.einsum(
        "gd,jdc->jgc", group_rows, whole_head, preferred_element_type=jnp.float32
    )
    bias_values = whole_bias.astype(jnp.float32)
    query_low = (projected[0] + bias_values[0]).astype(jnp.bfloat16)
    key_low = projected[1].astype(jnp.bfloat16)
    value_low = (projected[2] + bias_values[1]).astype(jnp.bfloat16)

    def shaped(array):
        return array.reshape(group_images, SEQ, heads_local, HEAD_DIM)

    query_img, key_img, value_img = (shaped(query_low), shaped(key_low), shaped(value_low))
    scores = scale * jnp.einsum(
        "ishd,ithd->ihst", query_img, key_img, preferred_element_type=jnp.float32
    )
    top_score = jnp.max(scores, axis=-1, keepdims=True)
    raised = jnp.exp(scores - top_score)
    row_total = jnp.sum(raised, axis=-1, keepdims=True)
    weights = raised / row_total
    log_total = top_score + jnp.log(row_total)
    attended = jnp.einsum(
        "ihst,ithd->ishd",
        weights.astype(jnp.bfloat16),
        value_img,
        preferred_element_type=jnp.float32,
    )
    attended_low = attended.reshape(group_count, head_cols).astype(jnp.bfloat16)
    segment = attended_low
    branch = lax.psum_scatter(
        jnp.dot(segment, whole_merge, preferred_element_type=jnp.float32).astype(jnp.bfloat16),
        "heads",
        scatter_dimension=0,
        tiled=True,
    ).astype(jnp.float32) + merge_bias.astype(jnp.float32)
    residual = residual_in + branch
    normed_two, norm_two_back = jax.vjp(
        layer_norm, residual, second_gain.astype(jnp.float32), second_bias.astype(jnp.float32)
    )
    second_low = normed_two.astype(jnp.bfloat16)
    router_logits = jnp.dot(second_low, router, preferred_element_type=jnp.float32) + router_noise
    chances = jax.nn.softmax(router_logits, axis=-1)
    expert_range = jnp.arange(experts, dtype=jnp.int32)
    chosen_pair = (expert_ids[:, :, None] == expert_range).astype(jnp.int32)
    chosen = jnp.sum(chosen_pair, axis=1)
    before = jnp.cumsum(chosen, axis=0) - chosen
    slot_ids = jnp.take_along_axis(before, expert_ids, axis=1)
    flat_rows = (slot_ids * experts + expert_ids).reshape(-1)
    picks = chosen_pair.astype(jnp.float32)
    count_terms = jnp.sum(chosen.astype(jnp.float32), axis=0)
    chance_terms = jnp.sum(chances, axis=0)
    count_all, chance_all = lax.psum((count_terms, chance_terms), ("dp", "heads", "tensor"))
    load_share = count_all / (2 * total_tokens)
    balance_loss = experts * jnp.sum(load_share * chance_all / total_tokens)
    gate_values = jnp.sum(picks * chances[:, None, :], axis=2)
    doubled = jnp.repeat(second_low, 2, axis=0)
    own_buffer = jnp.zeros((CAP * experts, features), jnp.bfloat16).at[flat_rows].set(doubled)
    pair_buffer = lax.all_gather(
        own_buffer.reshape(CAP, experts, features), "tensor", axis=0, tiled=True
    )
    weight_in, weight_out, bias_in = expert_weights(expert_in, expert_out, expert_in_bias)
    before_act = (
        jnp.einsum("ced,edf->cef", pair_buffer, weight_in, preferred_element_type=jnp.float32)
        + bias_in.astype(jnp.float32)[None, :, :]
    )
    activated, gelu_back = jax.vjp(jax.nn.gelu, before_act)
    activated_low = activated.astype(jnp.bfloat16)
    partial_out = jnp.einsum(
        "cef,efd->ced", activated_low, weight_out, preferred_element_type=jnp.float32
    )
    own_out = (
        lax.psum_scatter(
            partial_out.astype(jnp.bfloat16), "tensor", scatter_dimension=0, tiled=True
        ).astype(jnp.float32)
        + expert_out_bias.astype(jnp.float32)[None, :, :]
    )
    picked = own_out.reshape(CAP * experts, features)[flat_rows].reshape(tok_rows, 2, features)
    output = residual + jnp.sum(gate_values[:, :, None] * picked, axis=1)
    incoming = cotangent.astype(jnp.float32)
    gate_grad = jnp.sum(incoming[:, None, :] * picked, axis=2)
    slot_grad = (
        (gate_values[:, :, None] * incoming[:, None, :])
        .astype(jnp.bfloat16)
        .reshape(tok_rows * 2, features)
    )
    own_slot_grad = (
        jnp.zeros((CAP * experts, features), jnp.bfloat16)
        .at[flat_rows]
        .set(slot_grad)
        .reshape(CAP, experts, features)
    )
    out_bias_grad = jnp.sum(own_slot_grad, axis=0, dtype=jnp.float32)
    pair_grad = lax.all_gather(own_slot_grad, "tensor", axis=0, tiled=True)
    back_in, back_out, unused_bias = expert_weights(expert_in, expert_out, expert_in_bias)
    hidden_grad = jnp.einsum(
        "ced,efd->cef", pair_grad, back_out, preferred_element_type=jnp.float32
    )
    pre_grad = gelu_back(hidden_grad)[0].astype(jnp.bfloat16)
    out_grad_rows = jnp.einsum(
        "cef,ced->def", activated_low, pair_grad, preferred_element_type=jnp.float32
    )
    in_grad_rows = jnp.einsum(
        "ced,cef->def", pair_buffer, pre_grad, preferred_element_type=jnp.float32
    )
    in_bias_rows = jnp.sum(pre_grad, axis=0, dtype=jnp.float32).T
    in_grad_rows, out_grad_rows, in_bias_rows = (
        lax.psum_scatter(in_grad_rows, ("dp", "heads"), scatter_dimension=0, tiled=True),
        lax.psum_scatter(out_grad_rows, ("dp", "heads"), scatter_dimension=0, tiled=True),
        lax.psum_scatter(in_bias_rows, ("dp", "heads"), scatter_dimension=0, tiled=True),
    )
    expert_in_grad = jnp.transpose(in_grad_rows, (1, 0, 2))
    expert_out_grad = jnp.transpose(out_grad_rows, (1, 2, 0))
    in_bias_grad = in_bias_rows.T
    buffer_grad = jnp.einsum("cef,edf->ced", pre_grad, back_in, preferred_element_type=jnp.float32)
    own_buffer_grad = (
        lax.psum_scatter(
            buffer_grad.astype(jnp.bfloat16), "tensor", scatter_dimension=0, tiled=True
        )
        .astype(jnp.float32)
        .reshape(CAP * experts, features)
    )
    second_grad = jnp.sum(own_buffer_grad[flat_rows].reshape(tok_rows, 2, features), axis=1)
    chance_grad = (
        jnp.sum(picks * gate_grad[:, :, None], axis=1) + experts * load_share / total_tokens
    )
    logit_grad = chances * (chance_grad - jnp.sum(chances * chance_grad, axis=-1, keepdims=True))
    logit_low = logit_grad.astype(jnp.bfloat16)
    router_grad = lax.dot_general(
        second_low, logit_low, (((0,), (0,)), ((), ())), preferred_element_type=jnp.float32
    )
    second_grad = second_grad + jnp.dot(logit_low, router.T, preferred_element_type=jnp.float32)
    resid_part, gain_two_grad, bias_two_grad = norm_two_back(second_grad)
    resid_grad = incoming + resid_part
    branch_low = resid_grad.astype(jnp.bfloat16)
    merge_bias_grad = jnp.sum(branch_low, axis=0, dtype=jnp.float32)
    group_grad = lax.all_gather(branch_low, "heads", axis=0, tiled=True)
    merge_rows_grad = lax.dot_general(
        group_grad, attended_low, (((0,), (0,)), ((), ())), preferred_element_type=jnp.float32
    )
    attended_grad = shaped(
        jnp.dot(group_grad, whole_merge.T, preferred_element_type=jnp.float32).astype(jnp.bfloat16)
    )
    weights_again = jnp.exp(
        scale
        * jnp.einsum("ishd,ithd->ihst", query_img, key_img, preferred_element_type=jnp.float32)
        - log_total
    )
    value_grad = jnp.einsum(
        "ihst,ishd->ithd",
        weights_again.astype(jnp.bfloat16),
        attended_grad,
        preferred_element_type=jnp.float32,
    )
    weight_grad = jnp.einsum(
        "ishd,ithd->ihst", attended_grad, value_img, preferred_element_type=jnp.float32
    )
    inner_sum = jnp.sum(weight_grad * weights_again, axis=-1, keepdims=True)
    score_low = (weights_again * (weight_grad - inner_sum)).astype(jnp.bfloat16)
    query_grad = scale * jnp.einsum(
        "ihst,ithd->ishd", score_low, key_img, preferred_element_type=jnp.float32
    )
    key_grad = scale * jnp.einsum(
        "ihst,ishd->ithd", score_low, query_img, preferred_element_type=jnp.float32
    )
    triple_low = jnp.stack(
        [
            query_grad.reshape(group_count, head_cols),
            key_grad.reshape(group_count, head_cols),
            value_grad.reshape(group_count, head_cols),
        ],
        axis=0,
    ).astype(jnp.bfloat16)
    head_rows_grad = jnp.einsum(
        "gd,jgc->djc", group_rows, triple_low, preferred_element_type=jnp.float32
    )
    head_bias_rows = jnp.sum(triple_low[0::2], axis=1, dtype=jnp.float32).T
    segment = triple_low
    first_grad = lax.psum_scatter(
        jnp.einsum("jgc,jdc->gd", segment, whole_head, preferred_element_type=jnp.float32).astype(
            jnp.bfloat16
        ),
        "heads",
        scatter_dimension=0,
        tiled=True,
    ).astype(jnp.float32)
    input_part, gain_one_grad, bias_one_grad = norm_back(first_grad)
    input_grad = resid_grad + input_part
    head_rows_grad, merge_rows_grad, head_bias_rows = (
        lax.psum_scatter(head_rows_grad, ("dp", "tensor"), scatter_dimension=0, tiled=True),
        lax.psum_scatter(merge_rows_grad, ("dp", "tensor"), scatter_dimension=0, tiled=True),
        lax.psum_scatter(head_bias_rows, ("dp", "tensor"), scatter_dimension=0, tiled=True),
    )
    head_weight_grad = jnp.transpose(head_rows_grad, (1, 0, 2))
    merge_grad = merge_rows_grad.T
    head_bias_grad = head_bias_rows.T
    small = lax.psum(
        (
            gain_one_grad,
            bias_one_grad,
            gain_two_grad,
            bias_two_grad,
            merge_bias_grad,
            router_grad,
            out_bias_grad,
        ),
        ("dp", "heads", "tensor"),
    )
    return (
        output,
        balance_loss,
        input_grad,
        small[0],
        small[1],
        head_weight_grad,
        head_bias_grad,
        merge_grad,
        small[4],
        small[2],
        small[3],
        small[5],
        expert_in_grad,
        in_bias_grad,
        expert_out_grad,
        small[6],
    )


def solution(mesh):
    in_specs = (
        P(("dp", "heads", "tensor"), None),
        P(),
        P(),
        P(None, ("dp", "tensor"), "heads"),
        P(None, ("heads", "dp", "tensor")),
        P("heads", ("dp", "tensor")),
        P(),
        P(),
        P(),
        P(),
        P(("dp", "heads", "tensor"), None),
        P(("dp", "heads", "tensor"), None),
        P(None, ("dp", "heads"), "tensor"),
        P(None, ("tensor", "dp", "heads")),
        P(None, "tensor", ("dp", "heads")),
        P(),
        P(("dp", "heads", "tensor"), None),
    )
    out_specs = (
        P(("dp", "heads", "tensor"), None),
        P(),
        P(("dp", "heads", "tensor"), None),
        P(),
        P(),
        P(None, ("dp", "tensor"), "heads"),
        P(None, ("heads", "dp", "tensor")),
        P("heads", ("dp", "tensor")),
        P(),
        P(),
        P(),
        P(),
        P(None, ("dp", "heads"), "tensor"),
        P(None, ("tensor", "dp", "heads")),
        P(None, "tensor", ("dp", "heads")),
        P(),
    )
    return jax.shard_map(body, mesh=mesh, in_specs=in_specs, out_specs=out_specs, check_vma=False)
```

profile of v0, /device:TPU:0, one launch (start us, length us, event | category | flops | bytes accessed | tf_op | source)
XLA Modules:
  0.0 1218.7 jit_solution(1712219067057336657)
XLA Ops:
  15.9 22.3 %all-gather.1 = bf16[8,24,2]{1,2,0:T(2,128)(2,1)S(1)} all-gather(bf16[1,24,2]{1,2,0:T(2,128)(2,1)} %bitcast.169), channel_id=1, replica_groups=mesh['dp'=4,'heads'=4,'tensor'=2] {'dp','tensor'}, dimensions={0}, use_global_device_ids=true | all-gather | bytes 864 | tf_op jit(solution)/shard_map/all_gather | solution.py:55
  40.4 5.9 gather_fusion.2
  47.0 35.3 %all_gather.33 = bf16[3,768,192]{2,0,1:T(4,128)(2,1)S(1)} all-gather(bf16[3,96,192]{2,0,1:T(4,128)(2,1)S(1)} %copy.207), channel_id=1, replica_groups=mesh['dp'=4,'heads'=4,'tensor'=2] {'dp','tensor'}, dimensions={1}, use_global_device_ids=true | all-gather | bytes 995328 | tf_op jit(solution)/shard_map/all_gather | solution.py:53
  83.2 31.2 %all_gather.35 = bf16[192,768]{0,1:T(8,128)(2,1)S(1)} all-gather(bf16[192,96]{0,1:T(8,128)(2,1)S(1)} %copy.215), channel_id=1, replica_groups=mesh['dp'=4,'heads'=4,'tensor'=2] {'dp','tensor'}, dimensions={1}, use_global_device_ids=true | all-gather | bytes 331776 | tf_op jit(solution)/shard_map/all_gather | solution.py:54
  122.4 15.6 %fusion = bf16[200,768]{1,0:T(8,128)(2,1)S(1)} fusion(bf16[788,768]{1,0:T(8,128)(2,1)S(1)} %convolution_convert_fusion.2), kind=kCustom, calls=%all-reduce-scatter | all-reduce-scatter fusion | flops 614401 | bytes 1518080
  149.2 20.0 %all-gather.2 = bf16[16,96,4]{1,2,0:T(4,128)(2,1)S(1)} all-gather(bf16[1,96,4]{1,2,0:T(4,128)(2,1)S(1)} %bitcast.168), channel_id=1, replica_groups=mesh['dp'=4,'heads'=4,'tensor'=2] {'dp','heads'}, dimensions={0}, use_global_device_ids=true | all-gather | bytes 13056 | tf_op jit(solution)/shard_map/all_gather | solution.py:22
  172.2 2.5 scatter_custom_fusion.1
  176.4 83.7 %all-gather.13.cloned.1.call-done = bf16[4,768,1536]{2,1,0:T(8,128)(2,1)} async-done(((bf16[4,48,1536]{2,1,0:T(8,128)(2,1)}), bf16[4,768,1536]{2,1,0:T(8,128)(2,1)}) %all-gather.13.cloned.1.call-update) | async-done | bytes 9437200 | tf_op jit(solution)/shard_map/all_gather | solution.py:20
  260.1 9.4 fusion.79
  269.5 72.4 %all-gather.15.cloned.1.call-done = bf16[4,1536,768]{1,2,0:T(8,128)(2,1)} async-done(((bf16[4,1536,48]{1,2,0:T(8,128)(2,1)}), bf16[4,1536,768]{1,2,0:T(8,128)(2,1)}) %all-gather.15.cloned.1.call-update) | async-done | bytes 9437200 | tf_op jit(solution)/shard_map/all_gather | solution.py:21
  341.9 9.9 fusion.15
  351.8 17.4 %all-gather.17.cloned.1.call-done = bf16[256,4,768]{2,0,1:T(8,128)(2,1)} async-done(((bf16[128,4,768]{2,0,1:T(8,128)(2,1)}), bf16[256,4,768]{2,0,1:T(8,128)(2,1)}) %all-gather.17.cloned.1.call-update) | async-done | bytes 1572880 | tf_op jit(solution)/shard_map/all_gather | solution.py:155
  369.2 10.1 convert_reduce_fusion
  380.9 10.9 fusion.16
  392.0 39.5 %psum.63 = f32[4]{0:T(128)S(1)} all-reduce(f32[4]{0:T(128)S(1)} %convert_reduce_fusion.7), channel_id=1, replica_groups=mesh['dp'=4,'heads'=4,'tensor'=2] {'dp','heads','tensor'}, use_global_device_ids=true, to_apply=%region_17.18 | all-reduce | flops 4 | bytes 32 | tf_op jit(solution)/shard_map/psum | solution.py:114
  441.6 4.5 multiply_reduce_fusion.2
  446.2 2.9 copy.227
  462.6 17.0 %all-gather.21.cloned.1.call-done = bf16[4,197,768]{2,1,0:T(8,128)(2,1)} async-done(((bf16[1,197,768]{2,1,0:T(8,128)(2,1)}), bf16[4,197,768]{2,1,0:T(8,128)(2,1)}) %all-gather.21.cloned.1.call-update) | async-done | bytes 1210384 | tf_op jit(solution)/shard_map/all_gather | solution.py:198
  481.2 2.7 fusion.81
  484.1 11.1 convolution_bitcast_fusion.1
  495.1 22.7 %copy.240 = f32[768,4,1536]{2,1,0:T(4,128)} copy(f32[768,4,1536]{0,2,1:T(8,128)} %convolution_bitcast_fusion.1) | data formatting | bytes 37748736 | tf_op jit(solution)/shard_map/ced,cef->def/transpose | solution.py:164
  517.9 2.8 reshape.300
  520.8 2.7 convolution_convert_fusion.5
  538.8 4.2 fusion.80
  544.4 12.0 convolution_bitcast_fusion
  561.7 2.7 bitcast_convert_fusion
  564.4 15.8 %fusion.1 = bf16[200,768]{1,0:T(8,128)(2,1)S(1)} fusion(bf16[788,768]{1,0:T(8,128)(2,1)S(1)} %bitcast_convert_fusion), kind=kCustom, calls=%all-reduce-scatter.1 | all-reduce-scatter fusion | flops 614401 | bytes 1518080
  582.8 21.4 %all-reduce.3 = f32[192,2]{0,1:T(2,128)S(1)} all-reduce(f32[192,2]{0,1:T(2,128)S(1)} %bitcast.161), channel_id=7, replica_groups=mesh['dp'=4,'heads'=4,'tensor'=2] {'dp','tensor'}, use_global_device_ids=true, to_apply=%region_39.40.clone | all-reduce | flops 384 | bytes 3072
  607.4 39.9 %all-reduce.7 = (f32[4]{0:T(128)S(1)}, f32[768]{0:T(1024)}, f32[768]{0:T(1024)}, f32[768]{0:T(1024)}, f32[768]{0:T(1024)}, /*index=5*/f32[768]{0:T(1024)}, f32[768,4]{0,1:T(4,128)}, f32[4,768]{1,0:T(4,128)}) all-reduce(f32[4]{0:T(128)S(1)} %get-tuple-element.121, ...), channel_id=1, replica_groups=mesh['dp'=4,'heads'=4,'tensor'=2] {'dp','heads','tensor'}, use_global_device_ids=true, to_apply=%region_19.20 | all-reduce | flops 9988 | bytes 79904 | tf_op jit(solution)/shard_map/psum | solution.py:114
  650.2 287.7 %all-reduce.10.cloned.1.call-done = f32[768,4,1536]{2,1,0:T(4,128)} async-done(((f32[768,4,1536]{2,1,0:T(4,128)}), f32[768,4,1536]{2,1,0:T(4,128)}) %all-reduce.10.cloned.1.call-update) | async-done | bytes 18874384
  940.6 70.8 %reduce-scatter.18.cloned.1.call-done = f32[96,3,192]{2,0,1:T(8,128)} async-done(((f32[768,3,192]{2,0,1:T(8,128)}), f32[96,3,192]{2,0,1:T(8,128)}) %reduce-scatter.18.cloned.1.call-update) | async-done | bytes 221200 | tf_op jit(solution)/shard_map/reduce_scatter | solution.py:251
  1011.4 199.2 %reduce-scatter.22.cloned.1.call-done = f32[48,4,1536]{2,0,1:T(8,128)} async-done(((f32[768,4,1536]{2,0,1:T(8,128)}), f32[48,4,1536]{2,0,1:T(8,128)}) %reduce-scatter.22.cloned.1.call-update) | async-done | bytes 1179664 | tf_op jit(solution)/shard_map/reduce_scatter | solution.py:170
  (329 shorter events, 93.0 us)
Async XLA Ops:
  7.2 163.4 %copy-start = (bf16[768,4]{0,1:T(4,128)(2,1)S(1)}, bf16[768,4]{0,1:T(4,128)(2,1)}, u32[]{:S(2)}) copy-start(bf16[768,4]{0,1:T(4,128)(2,1)} %param.26) | copy-start | bytes 18436
  7.2 107.1 %all-gather.19.cloned.1.call-start = ((), (), s32[]{:S(2)}) async-start(), calls=%async_computation.15 | async-start | bytes 1536000 | tf_op jit(solution)/shard_map/all_gather | solution.py:61
  8.3 31.0 %copy-start.41 = (f32[197]{0:T(256)}, f32[197]{0:T(256)S(1)}, u32[]{:S(2)}) copy-start(f32[197]{0:T(256)S(1)} %broadcast_multiply_fusion.1) | copy-start | bytes 2368
  10.8 29.2 %copy-start.33 = (f32[768]{0:T(1024)}, f32[768]{0:T(1024)S(1)}, u32[]{:S(2)}) copy-start(f32[768]{0:T(1024)S(1)} %convert_element_type.137) | copy-start | bytes 9220
  13.5 162.9 %all-gather.11.cloned.1.call-start = ((), (), s32[]{:S(2)}) async-start(), calls=%async_computation.6 | async-start | bytes 2359296 | tf_op jit(solution)/shard_map/all_gather | solution.py:120
  38.4 81.8 %copy-start.63 = (f32[3,64]{1,0:T(4,128)}, f32[3,64]{1,0:T(4,128)S(1)}, u32[]{:S(2)}) copy-start(f32[3,64]{1,0:T(4,128)S(1)} %add.193) | copy-start | bytes 2308
  38.5 80.6 %copy-start.46 = (f32[3,64]{1,0:T(4,128)}, f32[3,64]{1,0:T(4,128)S(1)}, u32[]{:S(2)}) copy-start(f32[3,64]{1,0:T(4,128)S(1)} %add.196) | copy-start | bytes 2308
  83.2 34.0 %copy-start.27 = (bf16[3,768,192]{1,2,0:T(8,128)(2,1)}, bf16[3,768,192]{1,2,0:T(8,128)(2,1)S(1)}, u32[]{:S(2)}) copy-start(bf16[3,768,192]{1,2,0:T(8,128)(2,1)S(1)} %copy.208) | copy-start | bytes 2654212
  138.0 2.9 collective-permute-start
  146.6 22.7 %copy-start.14 = (bf16[197,768]{1,0:T(8,128)(2,1)S(1)}, bf16[197,768]{1,0:T(8,128)(2,1)}, u32[]{:S(2)}) copy-start(bf16[197,768]{1,0:T(8,128)(2,1)} %param.33) | copy-start | bytes 907780
  147.8 112.2 %all-gather.13.cloned.1.call-start = ((), (), s32[]{:S(2)}) async-start(), calls=%async_computation.7 | async-start | bytes 10027008 | tf_op jit(solution)/shard_map/all_gather | solution.py:20
  148.6 193.3 %all-gather.15.cloned.1.call-start = ((), (), s32[]{:S(2)}) async-start(), calls=%async_computation.8 | async-start | bytes 10027008 | tf_op jit(solution)/shard_map/all_gather | solution.py:21
  149.2 23.0 %copy-start.66 = (s32[394,1]{0,1:T(1,128)S(1)}, s32[394,1]{0,1:T(1,128)}, u32[]{:S(2)}) copy-start(s32[394,1]{0,1:T(1,128)} %copy-done.65) | copy-start | bytes 4732
  149.2 220.0 %all-gather.17.cloned.1.call-start = ((), (), s32[]{:S(2)}) async-start(), calls=%async_computation.10 | async-start | bytes 2359296 | tf_op jit(solution)/shard_map/all_gather | solution.py:155
  169.4 199.8 %copy-start.28 = (f32[1536,4]{0,1:T(4,128)}, f32[1536,4]{0,1:T(4,128)S(1)}, u32[]{:S(2)}) copy-start(f32[1536,4]{0,1:T(4,128)S(1)} %reshape.296) | copy-start | bytes 73732
  174.8 94.6 %copy-start.8 = (bf16[128,4,768]{2,1,0:T(4,128)(2,1)}, bf16[128,4,768]{2,1,0:T(4,128)(2,1)S(1)}, u32[]{:S(2)}) copy-start(bf16[128,4,768]{2,1,0:T(4,128)(2,1)S(1)} %reshape.237) | copy-start | bytes 2359300
  175.9 257.6 %reduce-scatter.14.cloned.1.call-start = ((), (), s32[]{:S(2)}) async-start(), calls=%async_computation.9 | async-start | bytes 2359296 | tf_op jit(solution)/shard_map/reduce_scatter | solution.py:134
  351.8 94.5 %reduce-scatter.16.cloned.1.call-start = ((), (), s32[]{:S(2)}) async-start(), calls=%async_computation.11 | async-start | bytes 2359296 | tf_op jit(solution)/shard_map/reduce_scatter | solution.py:178
  391.8 40.6 %copy-start.67 = (bf16[4,768]{1,0:T(4,128)(2,1)S(1)}, bf16[4,768]{1,0:T(4,128)(2,1)}, u32[]{:S(2)}) copy-start(bf16[4,768]{1,0:T(4,128)(2,1)} %param.32) | copy-start | bytes 18436
  391.9 87.8 %all-gather.21.cloned.1.call-start = ((), (), s32[]{:S(2)}) async-start(), calls=%async_computation.16 | async-start | bytes 1536000 | tf_op jit(solution)/shard_map/all_gather | solution.py:198
  461.0 99.0 %reduce-scatter.24.cloned.1.call-start = ((), (), s32[]{:S(2)}) async-start(), calls=%async_computation.17 | async-start | bytes 835584
  462.3 186.2 %reduce-scatter.20.cloned.1.call-start = ((), (), s32[]{:S(2)}) async-start(), calls=%async_computation.13 | async-start | bytes 884736 | tf_op jit(solution)/shard_map/reduce_scatter | solution.py:252
  484.0 453.9 %all-reduce.10.cloned.1.call-start = ((), (), s32[]{:S(2)}) async-start(), calls=%async_computation.18 | async-start | bytes 37748736
  517.9 493.5 %reduce-scatter.18.cloned.1.call-start = ((), (), s32[]{:S(2)}) async-start(), calls=%async_computation.12 | async-start | bytes 2654208 | tf_op jit(solution)/shard_map/reduce_scatter | solution.py:251
  543.0 667.6 %reduce-scatter.22.cloned.1.call-start = ((), (), s32[]{:S(2)}) async-start(), calls=%async_computation.14 | async-start | bytes 20054016 | tf_op jit(solution)/shard_map/reduce_scatter | solution.py:170
  564.3 41.0 %copy-start.34 = (f32[768]{0:T(1024)S(1)}, f32[768]{0:T(1024)}, u32[]{:S(2)}) copy-start(f32[768]{0:T(1024)} %copy-done.33) | copy-start | bytes 9220
  564.3 41.0 %copy-start.42 = (f32[197]{0:T(256)S(1)}, f32[197]{0:T(256)}, u32[]{:S(2)}) copy-start(f32[197]{0:T(256)} %copy-done.41) | copy-start | bytes 2368
  564.4 41.3 %copy-start.58 = (f32[197]{0:T(256)S(1)}, f32[197]{0:T(256)}, u32[]{:S(2)}) copy-start(f32[197]{0:T(256)} %copy-done.57) | copy-start | bytes 2368
  564.4 41.3 %copy-start.49 = (f32[197]{0:T(256)S(1)}, f32[197]{0:T(256)}, u32[]{:S(2)}) copy-start(f32[197]{0:T(256)} %copy-done.48) | copy-start | bytes 2368
  564.4 41.8 %copy-start.13 = (f32[197,768]{1,0:T(8,128)S(1)}, f32[197,768]{1,0:T(8,128)}, u32[]{:S(2)}) copy-start(f32[197,768]{1,0:T(8,128)} %copy-done.12) | copy-start | bytes 1815556
  580.2 67.0 %copy-start.78 = (f32[4]{0:T(128)S(1)}, f32[4]{0:T(128)}, u32[]{:S(2)}) copy-start(f32[4]{0:T(128)} %copy-done.77) | copy-start | bytes 52
  580.2 24.6 %collective-permute-start.1 = (bf16[9,768]{1,0:T(8,128)(2,1)S(1)}, bf16[9,768]{1,0:T(8,128)(2,1)S(1)}, u32[]{:S(2)}, u32[]{:S(2)}) collective-permute-start(bf16[9,768]{1,0:T(8,128)(2,1)S(1)} %slice.51), channel_id=1, source_target_pairs={{0,2},{2,4},{4,6},{1,3},{3,5},{5,7},{8,10},{10,12},{12,14},{9,11},... | collective-permute-start | bytes 41480
  (62 other events, 335.9 us)
Sparse Core Ops, SparseCore 0:
  13.6 20.4 all-gather.18
  148.0 28.2 all-gather.10
  178.6 81.4 all-gather.12
  262.2 79.5 all-gather.14
  343.8 25.3 all-gather.16
  371.3 26.0 reduce-scatter.13
  399.8 26.2 reduce-scatter.15
  461.2 18.4 all-gather.20
  483.2 56.5 reduce-scatter.23
  543.2 61.5 reduce-scatter.19
  608.7 329.1 all-reduce.9
  942.2 69.1 reduce-scatter.17
  1016.6 193.9 reduce-scatter.21
where the time goes:
time: 1230 us; the launch traced here: 1220 us
  waiting for transfers between devices  750 us (61%)
  blocking collectives  241 us (20%)
  matrix products  87.8 us (7%)
  local copies, waits for them, and re-layouts  87 us (7%)
  other arithmetic  29.6 us (2%)
  between operations  19.5 us (2%)
    unnamed x17, waiting for transfers between devices  289 us
    reduce_scatter x1, waiting for transfers between devices, body(): lax.psum_scatter(out_grad_rows, ('dp', 'heads'), scatter_dimension=0, til...  199 us
    all_gather x1, waiting for transfers between devices, expert_weights(): lax.all_gather(expert_in, ('dp', 'heads'), axis=1, tiled=True)  83.7 us
    psum x2, blocking collectives, body(): lax.psum((count_terms, chance_terms), ('dp', 'heads', 'tensor'))  79.4 us
    all_gather x1, waiting for transfers between devices, expert_weights(): lax.all_gather(expert_out, ('dp', 'heads'), axis=2, tiled=True)  72.4 us
    reduce_scatter x1, waiting for transfers between devices, body(): lax.psum_scatter(head_rows_grad, ('dp', 'tensor'), scatter_dimension=0, t...  70.8 us
    unnamed x3, blocking collectives  52.7 us
    all_gather x1, blocking collectives, body(): lax.all_gather(head_weight, ('dp', 'tensor'), axis=1, tiled=True)  35.3 us
  transfers between devices with their start and end apart: 15, of which 7 were waited for; matrix products, arithmetic and copies ran while one was open for 15% of the time, Pallas kernels for 0%

commit v1 on v0

--- a/solution.py
+++ b/solution.py
@@ -1,11 +1,857 @@
+import functools
+
 import jax
 import jax.numpy as jnp
 from jax import lax
+from jax.experimental import pallas as pl
+from jax.experimental.pallas import tpu as pltpu
 from jax.sharding import PartitionSpec as P
 
 HEAD_DIM = 64
 SEQ = 197
 CAP = 128
+ROWS = 208
+MIB = 1 << 20
+F32 = jnp.float32
+BF16 = jnp.bfloat16
+VM = pl.BlockSpec(memory_space=pltpu.VMEM)
+ANY = pl.BlockSpec(memory_space=pl.ANY)
+CHUNKS = (0, 1, 3, 4, 2, 8, 5, 11, 6, 7, 9, 10)
+
+
+def nn(a, b):
+    return lax.dot_general(a, b, (((1,), (0,)), ((), ())), preferred_element_type=F32)
+
+
+def nt(a, b):
+    return lax.dot_general(a, b, (((1,), (1,)), ((), ())), preferred_element_type=F32)
+
+
+def tn(a, b):
+    return lax.dot_general(a, b, (((0,), (0,)), ((), ())), preferred_element_type=F32)
+
+
+def place():
+    d, h, t = lax.axis_index("dp"), lax.axis_index("heads"), lax.axis_index("tensor")
+    return d, h // 2, h % 2, t
+
+
+def device(d, x, c, t):
+    return (d, 2 * x + c, t)
+
+
+def meet(peers):
+    barrier = pltpu.get_barrier_semaphore()
+    for peer in peers:
+        pl.semaphore_signal(barrier, inc=1, device_id=peer, device_id_type=pl.DeviceIdType.MESH)
+    pl.semaphore_wait(barrier, len(peers))
+
+
+def send(src, dst, send_sem, recv_sem, peer):
+    copy = pltpu.make_async_remote_copy(
+        src_ref=src,
+        dst_ref=dst,
+        send_sem=send_sem,
+        recv_sem=recv_sem,
+        device_id=peer,
+        device_id_type=pl.DeviceIdType.MESH,
+    )
+    copy.start()
+    return copy
+
+
+def planar(x, t):
+    return ((1 - x, t), (x, 1 - t), (1 - x, 1 - t))
+
+
+def gather_kernel(a_ref, w_ref, g_ref, e_ref, own_sem, zs, zr, ps, pr, cs, cr, ezs, ezr, exs, exr, ecs, ecr):
+    d, x, c, t = place()
+    plane = planar(x, t)
+    mate = device(d, x, 1 - c, t)
+    peers = [device((d + k) % 4, x, c, t) for k in (1, 2, 3)]
+    peers += [device(d, px, c, pt) for px, pt in plane] + [mate]
+    me = 2 * x + c
+    own = pltpu.make_async_copy(a_ref, g_ref.at[me, 2 * d + t], own_sem.at[0])
+    own.start()
+    own_w = pltpu.make_async_copy(w_ref.at[d], e_ref.at[:, 4 * d + me], own_sem.at[1])
+    own_w.start()
+    meet(peers)
+    sent = []
+
+    def slot(k, px, pt, pc):
+        return g_ref.at[2 * px + pc, 2 * ((d + 4 - k) % 4) + pt]
+
+    def piece(k, px, pc):
+        return e_ref.at[:, 4 * ((d + 4 - k) % 4) + 2 * px + pc]
+
+    for k in (1, 2, 3):
+        sent.append(send(a_ref, slot(0, x, t, c), zs.at[k - 1], zr.at[k - 1], device((d + k) % 4, x, c, t)))
+    for j, (px, pt) in enumerate(plane):
+        sent.append(send(a_ref, slot(0, x, t, c), ps.at[j, 0], pr.at[j, 0], device(d, px, c, pt)))
+    sent.append(send(a_ref, slot(0, x, t, c), cs.at[3, 0], cr.at[3, 0], mate))
+    for k in (1, 2, 3):
+        target = (d + k) % 4
+        sent.append(
+            send(w_ref.at[target], piece(0, x, c), ezs.at[k - 1], ezr.at[k - 1], device(target, x, c, t))
+        )
+    other = device(d, 1 - x, c, t)
+    sent.append(send(w_ref.at[d], piece(0, x, c), exs.at[0], exr.at[0], other))
+    sent.append(send(w_ref.at[d], piece(0, x, c), ecs.at[0, 0], ecr.at[0, 0], mate))
+    waits = []
+    for k in (1, 2, 3):
+        here = slot(k, x, t, c)
+        pltpu.make_async_copy(here, here, zr.at[k - 1]).wait()
+        for j, (px, pt) in enumerate(plane):
+            sent.append(send(here, here, ps.at[j, k], pr.at[j, k], device(d, px, c, pt)))
+        sent.append(send(here, here, cs.at[3, k], cr.at[3, k], mate))
+    for k in (1, 2, 3):
+        here = piece(k, x, c)
+        pltpu.make_async_copy(here, here, ezr.at[k - 1]).wait()
+        sent.append(send(here, here, exs.at[k], exr.at[k], other))
+        sent.append(send(here, here, ecs.at[0, k], ecr.at[0, k], mate))
+    for k in range(4):
+        for j, (px, pt) in enumerate(plane):
+            here = slot(k, px, pt, c)
+            pltpu.make_async_copy(here, here, pr.at[j, k]).wait()
+            sent.append(send(here, here, cs.at[j, k], cr.at[j, k], mate))
+    for k in range(4):
+        here = piece(k, 1 - x, c)
+        pltpu.make_async_copy(here, here, exr.at[k]).wait()
+        sent.append(send(here, here, ecs.at[1, k], ecr.at[1, k], mate))
+    for k in range(4):
+        for j, (px, pt) in enumerate(plane + ((x, t),)):
+            here = slot(k, px, pt, 1 - c)
+            pltpu.make_async_copy(here, here, cr.at[j, k]).wait()
+        for j, px in enumerate((x, 1 - x)):
+            here = piece(k, px, 1 - c)
+            pltpu.make_async_copy(here, here, ecr.at[j, k]).wait()
+    for copy in sent:
+        copy.wait_send()
+    own.wait()
+    own_w.wait()
+
+
+def gather_weights(shard, experts):
+    dma = pltpu.SemaphoreType.DMA
+    return pl.pallas_call(
+        gather_kernel,
+        out_shape=(
+            jax.ShapeDtypeStruct((4, 8) + shard.shape, BF16),
+            jax.ShapeDtypeStruct((2, 16) + experts.shape[2:], BF16),
+        ),
+        in_specs=[VM, VM],
+        out_specs=(ANY, ANY),
+        scratch_shapes=[
+            dma((2,)),
+            dma((3,)),
+            dma((3,)),
+            dma((3, 4)),
+            dma((3, 4)),
+            dma((4, 4)),
+            dma((4, 4)),
+            dma((3,)),
+            dma((3,)),
+            dma((4,)),
+            dma((4,)),
+            dma((2, 4)),
+            dma((2, 4)),
+        ],
+        compiler_params=pltpu.CompilerParams(collective_id=0, has_side_effects=True),
+        name="gather_weights",
+    )(shard, experts)
+
+
+def dispatch_kernel(s_ref, r_ref, own_sem, zs, zr, ys, yr):
+    d, x, c, t = place()
+    beside = device(d, x, c, 1 - t)
+    own = pltpu.make_async_copy(s_ref.at[d], r_ref.at[2 * d + t], own_sem)
+    own.start()
+    meet([device((d + k) % 4, x, c, t) for k in (1, 2, 3)] + [beside])
+    sent = []
+    for k in (1, 2, 3):
+        target = (d + k) % 4
+        sent.append(
+            send(s_ref.at[target], r_ref.at[2 * d + t], zs.at[k - 1], zr.at[k - 1], device(target, x, c, t))
+        )
+    sent.append(send(s_ref.at[d], r_ref.at[2 * d + t], ys.at[0], yr.at[0], beside))
+    for k in (1, 2, 3):
+        here = r_ref.at[2 * ((d + 4 - k) % 4) + t]
+        pltpu.make_async_copy(here, here, zr.at[k - 1]).wait()
+        sent.append(send(here, here, ys.at[k], yr.at[k], beside))
+    for k in range(4):
+        here = r_ref.at[2 * ((d + 4 - k) % 4) + 1 - t]
+        pltpu.make_async_copy(here, here, yr.at[k]).wait()
+    for copy in sent:
+        copy.wait_send()
+    own.wait()
+
+
+def dispatch(slots):
+    dma = pltpu.SemaphoreType.DMA
+    return pl.pallas_call(
+        dispatch_kernel,
+        out_shape=jax.ShapeDtypeStruct((8,) + slots.shape[1:], BF16),
+        in_specs=[VM],
+        out_specs=ANY,
+        scratch_shapes=[dma, dma((3,)), dma((3,)), dma((4,)), dma((4,))],
+        compiler_params=pltpu.CompilerParams(collective_id=1, has_side_effects=True),
+        name="dispatch_slots",
+    )(slots)
+
+
+def collect_kernel(p_ref, b_ref, got, acc, ys, yr, zs, zr):
+    d, x, c, t = place()
+    beside = device(d, x, c, 1 - t)
+    meet([device((d + k) % 4, x, c, t) for k in (1, 2, 3)] + [beside])
+    sent = []
+    order = [(d + k) % 4 for k in (1, 2, 3, 0)]
+    for k, z in enumerate(order):
+        sent.append(send(p_ref.at[2 * z + 1 - t], got.at[k], ys.at[k], yr.at[k], beside))
+    for k, z in enumerate(order):
+        pltpu.make_async_copy(got.at[k], got.at[k], yr.at[k]).wait()
+        total = (p_ref[2 * z + t].astype(F32) + got[k].astype(F32)).astype(BF16)
+        if k == 3:
+            b_ref[d] = total
+        else:
+            acc[k] = total
+            sent.append(send(acc.at[k], b_ref.at[d], zs.at[k], zr.at[k], device(z, x, c, t)))
+    for k in (1, 2, 3):
+        here = b_ref.at[(d + 4 - k) % 4]
+        pltpu.make_async_copy(here, here, zr.at[k - 1]).wait()
+    for copy in sent:
+        copy.wait_send()
+
+
+def collect(partial):
+    dma = pltpu.SemaphoreType.DMA
+    block = partial.shape[1:]
+    return pl.pallas_call(
+        collect_kernel,
+        out_shape=jax.ShapeDtypeStruct((4,) + block, BF16),
+        in_specs=[VM],
+        out_specs=VM,
+        scratch_shapes=[
+            pltpu.VMEM((4,) + block, BF16),
+            pltpu.VMEM((3,) + block, BF16),
+            dma((4,)),
+            dma((4,)),
+            dma((3,)),
+            dma((3,)),
+        ],
+        compiler_params=pltpu.CompilerParams(
+            collective_id=2, has_side_effects=True, vmem_limit_bytes=32 * MIB
+        ),
+        name="collect_rows",
+    )(partial)
+
+
+def reduce_experts_kernel(p_ref, o_ref, got1, acc1, got2, acc2, cs, cr, xs, xr, zs, zr):
+    d, x, c, t = place()
+    mate, other = device(d, x, 1 - c, t), device(d, 1 - x, c, t)
+    meet([device((d + k) % 4, x, c, t) for k in (1, 2, 3)] + [other, mate])
+    sent = []
+    order = [(d + k) % 4 for k in (1, 2, 3, 0)]
+    for i, px in enumerate((1 - x, x)):
+        for k, z in enumerate(order):
+            sent.append(
+                send(p_ref.at[:, 4 * z + 2 * px + 1 - c], got1.at[i, k], cs.at[i, k], cr.at[i, k], mate)
+            )
+    for i, px in enumerate((1 - x, x)):
+        for k, z in enumerate(order):
+            pltpu.make_async_copy(got1.at[i, k], got1.at[i, k], cr.at[i, k]).wait()
+            acc1[i, k] = (p_ref[:, 4 * z + 2 * px + c].astype(F32) + got1[i, k].astype(F32)).astype(BF16)
+            if i == 0:
+                sent.append(send(acc1.at[0, k], got2.at[k], xs.at[k], xr.at[k], other))
+    for k, z in enumerate(order):
+        pltpu.make_async_copy(got2.at[k], got2.at[k], xr.at[k]).wait()
+        total = (acc1[1, k].astype(F32) + got2[k].astype(F32)).astype(BF16)
+        if k == 3:
+            o_ref[d] = total
+        else:
+            acc2[k] = total
+            sent.append(send(acc2.at[k], o_ref.at[d], zs.at[k], zr.at[k], device(z, x, c, t)))
+    for k in (1, 2, 3):
+        here = o_ref.at[(d + 4 - k) % 4]
+        pltpu.make_async_copy(here, here, zr.at[k - 1]).wait()
+    for copy in sent:
+        copy.wait_send()
+
+
+def reduce_experts(partial):
+    dma = pltpu.SemaphoreType.DMA
+    two, _, rows, wide = partial.shape
+    piece = (two, rows, wide)
+    return pl.pallas_call(
+        reduce_experts_kernel,
+        out_shape=jax.ShapeDtypeStruct((4,) + piece, BF16),
+        in_specs=[VM],
+        out_specs=VM,
+        scratch_shapes=[
+            pltpu.VMEM((2, 4) + piece, BF16),
+            pltpu.VMEM((2, 4) + piece, BF16),
+            pltpu.VMEM((4,) + piece, BF16),
+            pltpu.VMEM((3,) + piece, BF16),
+            dma((2, 4)),
+            dma((2, 4)),
+            dma((4,)),
+            dma((4,)),
+            dma((3,)),
+            dma((3,)),
+        ],
+        compiler_params=pltpu.CompilerParams(
+            collective_id=3, has_side_effects=True, vmem_limit_bytes=48 * MIB
+        ),
+        name="reduce_experts",
+    )(partial)
+
+
+def reduce_shards_kernel(
+    p_ref, s_ref, o_ref, q_ref, got1, acc1, got2, acc2, got3, sgot, sacc, cs, cr, ps, pr, zs, zr, ss, sr
+):
+    d, x, c, t = place()
+    plane = planar(x, t)
+    mate = device(d, x, 1 - c, t)
+    along = [device((d + k) % 4, x, c, t) for k in (1, 2, 3)]
+    across = [device(d, px, c, pt) for px, pt in plane]
+    meet(along + across + [mate])
+    order = [(d + k) % 4 for k in (1, 2, 3, 0)]
+    columns = plane + ((x, t),)
+    sent = []
+    for j, (px, pt) in enumerate(columns):
+        for k, z in enumerate(order):
+            sent.append(
+                send(p_ref.at[2 * px + 1 - c, 2 * z + pt], got1.at[j, k], cs.at[j, k], cr.at[j, k], mate)
+            )
+    for k, peer in enumerate(along):
+        sent.append(send(s_ref, sgot.at[k], ss.at[k], sr.at[k], peer))
+    for j, (px, pt) in enumerate(columns):
+        for k, z in enumerate(order):
+            pltpu.make_async_copy(got1.at[j, k], got1.at[j, k], cr.at[j, k]).wait()
+            acc1[j, k] = (p_ref[2 * px + c, 2 * z + pt].astype(F32) + got1[j, k].astype(F32)).astype(BF16)
+            if j < 3:
+                sent.append(send(acc1.at[j, k], got2.at[j, k], ps.at[j, k], pr.at[j, k], across[j]))
+    for k in range(3):
+        pltpu.make_async_copy(sgot.at[k], sgot.at[k], sr.at[k]).wait()
+    sacc[0] = (s_ref[...] + sgot[1]) + (sgot[0] + sgot[2])
+    for k, peer in enumerate(across):
+        sent.append(send(sacc.at[0], sgot.at[3 + k], ss.at[3 + k], sr.at[3 + k], peer))
+    for k in range(4):
+        for j in range(3):
+            pltpu.make_async_copy(got2.at[j, k], got2.at[j, k], pr.at[j, k]).wait()
+        total = (acc1[3, k].astype(F32) + got2[0, k].astype(F32)) + (
+            got2[1, k].astype(F32) + got2[2, k].astype(F32)
+        )
+        acc2[k] = total.astype(BF16)
+        if k < 3:
+            sent.append(send(acc2.at[k], got3.at[k], zs.at[k], zr.at[k], along[k]))
+    for k in range(3):
+        pltpu.make_async_copy(sgot.at[3 + k], sgot.at[3 + k], sr.at[3 + k]).wait()
+    sacc[1] = (sacc[0] + sgot[5]) + (sgot[3] + sgot[4])
+    sent.append(send(sacc.at[1], sgot.at[6], ss.at[6], sr.at[6], mate))
+    for k in range(3):
+        pltpu.make_async_copy(got3.at[k], got3.at[k], zr.at[k]).wait()
+    o_ref[...] = (acc2[3].astype(F32) + got3[1].astype(F32)) + (got3[0].astype(F32) + got3[2].astype(F32))
+    pltpu.make_async_copy(sgot.at[6], sgot.at[6], sr.at[6]).wait()
+    q_ref[...] = sacc[1] + sgot[6]
+    for copy in sent:
+        copy.wait_send()
+
+
+def reduce_shards(partial, small):
+    dma = pltpu.SemaphoreType.DMA
+    block = partial.shape[2:]
+    return pl.pallas_call(
+        reduce_shards_kernel,
+        out_shape=(jax.ShapeDtypeStruct(block, F32), jax.ShapeDtypeStruct(small.shape, F32)),
+        in_specs=[VM, VM],
+        out_specs=(VM, VM),
+        scratch_shapes=[
+            pltpu.VMEM((4, 4) + block, BF16),
+            pltpu.VMEM((4, 4) + block, BF16),
+            pltpu.VMEM((3, 4) + block, BF16),
+            pltpu.VMEM((4,) + block, BF16),
+            pltpu.VMEM((3,) + block, BF16),
+            pltpu.VMEM((7,) + small.shape, F32),
+            pltpu.VMEM((2,) + small.shape, F32),
+            dma((4, 4)),
+            dma((4, 4)),
+            dma((3, 4)),
+            dma((3, 4)),
+            dma((3,)),
+            dma((3,)),
+            dma((7,)),
+            dma((7,)),
+        ],
+        compiler_params=pltpu.CompilerParams(
+            collective_id=4, has_side_effects=True, vmem_limit_bytes=48 * MIB
+        ),
+        name="reduce_shards",
+    )(partial, small)
+
+
+def normalise(values):
+    average = jnp.mean(values, axis=-1, keepdims=True)
+    centred = values - average
+    spread = jnp.mean(centred * centred, axis=-1, keepdims=True)
+    inverse = lax.rsqrt(spread + 1e-06)
+    return centred * inverse, inverse
+
+
+def lanes(shape):
+    return lax.broadcasted_iota(jnp.int32, shape, len(shape) - 1)
+
+
+def halves():
+    low = (lanes((1, 128)) < HEAD_DIM).astype(BF16)
+    return low, (1 - low.astype(F32)).astype(BF16)
+
+
+def selectors(spread_ref):
+    chosen = spread_ref[...]
+    rows = chosen.shape[1]
+    earlier = lax.broadcasted_iota(jnp.int32, (rows, rows), 0) < lanes((rows, rows))
+    before = nn(chosen.astype(BF16), earlier.astype(F32).astype(BF16)).astype(jnp.int32)
+    slot = lax.broadcasted_iota(jnp.int32, (CAP, rows), 0)
+    return [
+        jnp.where((before[e : e + 1] == slot) & (chosen[e : e + 1] > 0.5), 1.0, 0.0).astype(BF16)
+        for e in range(4)
+    ]
+
+
+HEADS_AT = ((0, 1, 4, 0, 0), (0, 1, 4, 1, 1), (2, 3, 2, 0, 1))
+
+
+def forward_kernel(
+    x_ref,
+    g_ref,
+    hb_ref,
+    vec_ref,
+    router_ref,
+    noise_ref,
+    spread_ref,
+    cot_ref,
+    n1_ref,
+    qkv_ref,
+    att_ref,
+    lse_ref,
+    res_ref,
+    ch_ref,
+    ds_ref,
+    ob_ref,
+):
+    rows, wide = x_ref.shape
+    values = x_ref[...].astype(F32)
+    normal, _ = normalise(values)
+    n1_ref[...] = (normal * vec_ref[0:1] + vec_ref[1:2]).astype(BF16)
+    res_ref[...] = values + vec_ref[4:5]
+    low, high = halves()
+    alive = lanes((1, rows)) < SEQ
+
+    def one(h, carry):
+        weight = g_ref[h, :, 0:96, :].reshape(wide, wide)
+        qkv_ref[h] = (nn(n1_ref[...], weight[:, 0:640]) + hb_ref[h]).astype(BF16)
+        parts = []
+        ends = jnp.zeros((rows, 128), F32)
+        for i, (sq, sk, sv, uq, uv) in enumerate(HEADS_AT):
+            query = qkv_ref[h, :, 128 * sq : 128 * sq + 128] * (high if uq else low)
+            key = qkv_ref[h, :, 128 * sk : 128 * sk + 128]
+            value = qkv_ref[h, :, 128 * sv : 128 * sv + 128] * (high if uv else low)
+            scores = jnp.where(alive, HEAD_DIM ** (-0.5) * nt(query, key), -1e30)
+            top = jnp.max(scores, axis=-1, keepdims=True)
+            raised = jnp.exp(scores - top)
+            total = jnp.sum(raised, axis=-1, keepdims=True)
+            parts.append(nn((raised / total).astype(BF16), value))
+            ends = jnp.where(lanes((1, 128)) == i, top + jnp.log(total), ends)
+        lse_ref[h] = ends
+        first, second = (parts[0] + parts[1]).astype(BF16), parts[2].astype(BF16)
+        att_ref[h, :, 0:128] = first
+        att_ref[h, :, 128:256] = second
+        res_ref[...] += nt(first, weight[:, 640:768]) + nt(second, weight[:, 384:512])
+        return carry
+
+    lax.fori_loop(0, 4, one, 0)
+    normal, _ = normalise(res_ref[...])
+    second = (normal * vec_ref[2:3] + vec_ref[3:4]).astype(BF16)
+    logits = nn(second, router_ref[...]) + noise_ref[...]
+    raised = jnp.exp(logits - jnp.max(logits, axis=-1, keepdims=True))
+    chances = raised / jnp.sum(raised, axis=-1, keepdims=True)
+    ch_ref[...] = chances
+    incoming = cot_ref[...].astype(F32)
+    for e, select in enumerate(selectors(spread_ref)):
+        ds_ref[e, 0] = nn(select, second).astype(BF16)
+        taken = nn(select, (chances[:, e : e + 1] * incoming).astype(BF16))
+        ds_ref[e, 1] = taken.astype(BF16)
+        ob_ref[e : e + 1] = jnp.sum(taken, axis=0, keepdims=True)
+    ob_ref[4:8] = jnp.zeros((4, wide), F32)
+
+
+def forward_block(x, gathered, bias, vectors, router, noise, spread, cot):
+    rows, wide = x.shape
+    return pl.pallas_call(
+        forward_kernel,
+        out_shape=(
+            jax.ShapeDtypeStruct((rows, wide), BF16),
+            jax.ShapeDtypeStruct((4, rows, 640), BF16),
+            jax.ShapeDtypeStruct((4, rows, 256), BF16),
+            jax.ShapeDtypeStruct((4, rows, 128), F32),
+            jax.ShapeDtypeStruct((rows, wide), F32),
+            jax.ShapeDtypeStruct((rows, 128), F32),
+            jax.ShapeDtypeStruct((4, 2, CAP, wide), BF16),
+            jax.ShapeDtypeStruct((8, wide), F32),
+        ),
+        in_specs=[VM] * 8,
+        out_specs=(VM,) * 8,
+        compiler_params=pltpu.CompilerParams(vmem_limit_bytes=48 * MIB),
+        cost_estimate=pl.CostEstimate(flops=2 * 10**9, bytes_accessed=12 * 10**6, transcendentals=10**6),
+        name="attention_forward",
+    )(x, gathered, bias, vectors, router, noise, spread, cot)
+
+
+def expert_kernel(r_ref, w_ref, b_ref, o_ref, dw_ref, db_ref, hid, pre, xt, rt):
+    blocks, _, cap, wide = r_ref.shape
+    units = w_ref.shape[3]
+    step, tile = 2 * cap, 512
+    db_ref[...] = jnp.zeros_like(db_ref)
+
+    def rows_of(i, carry):
+        x = r_ref[pl.ds(2 * i, 2), 0].reshape(step, wide)
+        r = r_ref[pl.ds(2 * i, 2), 1].reshape(step, wide)
+        at = pl.ds(pl.multiple_of(i * step, step), step)
+        xt[:, at] = x.T
+        rt[:, at] = r.T
+        out = jnp.zeros((step, wide), F32)
+        back = jnp.zeros((step, wide), F32)
+        for f in range(units // tile):
+            cols = slice(f * tile, f * tile + tile)
+            w_in = w_ref[0, :, :, cols].reshape(wide, tile)
+            w_out = w_ref[1, :, :, cols].reshape(wide, tile)
+            v = nn(x, w_in) + b_ref[0:1, cols]
+            square = v * v
+            bend = jnp.tanh(0.7978845608028654 * v * (1.0 + 0.044715 * square))
+            hidden = (0.5 * v * (1.0 + bend)).astype(BF16)
+            slope = 0.5 * (1.0 + bend) + 0.5 * v * (1.0 - bend * bend) * (
+                0.7978845608028654 * (1.0 + 3 * 0.044715 * square)
+            )
+            grad = nn(r, w_out) * slope
+            low = grad.astype(BF16)
+            hid[at, cols] = hidden
+            pre[at, cols] = low
+            db_ref[0:1, cols] += jnp.sum(low.astype(F32), axis=0, keepdims=True)
+            out += nt(hidden, w_out)
+            back += nt(low, w_in)
+        o_ref[pl.ds(2 * i, 2), 0] = out.astype(BF16).reshape(2, cap, wide)
+        o_ref[pl.ds(2 * i, 2), 1] = back.astype(BF16).reshape(2, cap, wide)
+        return carry
+
+    lax.fori_loop(0, blocks // 2, rows_of, 0)
+
+    def columns_of(f, carry):
+        cols = pl.ds(pl.multiple_of(f * 256, 256), 256)
+        shape = w_ref.shape[1:3] + (256,)
+        dw_ref[0, :, :, cols] = nn(xt[...], pre[:, cols]).astype(BF16).reshape(shape)
+        dw_ref[1, :, :, cols] = nn(rt[...], hid[:, cols]).astype(BF16).reshape(shape)
+        return carry
+
+    lax.fori_loop(0, units // 256, columns_of, 0)
+
+
+def expert_block(received, weights, bias):
+    blocks, _, cap, wide = received.shape
+    units = weights.shape[3]
+    return pl.pallas_call(
+        expert_kernel,
+        out_shape=(
+            jax.ShapeDtypeStruct(received.shape, BF16),
+            jax.ShapeDtypeStruct(weights.shape, BF16),
+            jax.ShapeDtypeStruct((8, units), F32),
+        ),
+        in_specs=[VM] * 3,
+        out_specs=(VM,) * 3,
+        scratch_shapes=[
+            pltpu.VMEM((blocks * cap, units), BF16),
+            pltpu.VMEM((blocks * cap, units), BF16),
+            pltpu.VMEM((wide, blocks * cap), BF16),
+            pltpu.VMEM((wide, blocks * cap), BF16),
+        ],
+        compiler_params=pltpu.CompilerParams(vmem_limit_bytes=56 * MIB),
+        cost_estimate=pl.CostEstimate(flops=15 * 10**9, bytes_accessed=16 * 10**6, transcendentals=2 * 10**6),
+        name="expert_block",
+    )(received, weights, bias)
+
+
+def backward_kernel(
+    x_ref,
+    g_ref,
+    vec_ref,
+    router_ref,
+    chosen_ref,
+    spread_ref,
+    cot_ref,
+    load_ref,
+    eb_ref,
+    n1_ref,
+    qkv_ref,
+    att_ref,
+    lse_ref,
+    res_ref,
+    ch_ref,
+    ob_ref,
+    bk_ref,
+    out_ref,
+    ig_ref,
+    dg_ref,
+    hb_ref,
+    sm_ref,
+    n1t,
+    brt,
+    dqkv,
+    dn1,
+):
+    rows, wide = x_ref.shape
+    incoming = cot_ref[...].astype(F32)
+    chances, chosen = ch_ref[...], chosen_ref[...]
+    normal, inverse = normalise(res_ref[...])
+    second = (normal * vec_ref[2:3] + vec_ref[3:4]).astype(BF16)
+    output = res_ref[...]
+    dn2 = jnp.zeros((rows, wide), F32)
+    gate_grads = jnp.zeros((rows, 128), F32)
+    for e, select in enumerate(selectors(spread_ref)):
+        used = chosen[:, e : e + 1]
+        picked = tn(select, bk_ref[e, 0]) + used * eb_ref[e : e + 1]
+        output += chances[:, e : e + 1] * picked
+        gate_grads = jnp.where(
+            lanes((1, 128)) == e, jnp.sum(incoming * picked, axis=-1, keepdims=True), gate_grads
+        )
+        dn2 += tn(select, bk_ref[e, 1])
+    out_ref[...] = output
+    chance_grad = gate_grads + load_ref[0:1]
+    logit_grad = chances * (chance_grad - jnp.sum(chances * chance_grad, axis=-1, keepdims=True))
+    living = lax.broadcasted_iota(jnp.int32, (rows, 1), 0) < SEQ
+    logit_low = jnp.where(living, logit_grad, 0.0).astype(BF16)
+    router_grad = tn(logit_low, second)
+    dn2 += nt(logit_low, router_ref[...])
+    scaled = dn2 * vec_ref[2:3]
+    resid = incoming + inverse * (
+        scaled
+        - jnp.mean(scaled, axis=-1, keepdims=True)
+        - normal * jnp.mean(scaled * normal, axis=-1, keepdims=True)
+    )
+    ig_ref[...] = resid
+    branch = resid.astype(BF16)
+    sm_ref[...] = jnp.zeros_like(sm_ref)
+    sm_ref[2:3] = jnp.sum(dn2 * normal, axis=0, keepdims=True)
+    sm_ref[3:4] = jnp.sum(dn2, axis=0, keepdims=True)
+    sm_ref[4:5] = jnp.sum(branch.astype(F32), axis=0, keepdims=True)
+    sm_ref[8:12] = router_grad[0:4]
+    sm_ref[12:16] = ob_ref[0:4]
+    sm_ref[5:6, 0:128] = jnp.sum(jnp.where(living, chances, 0.0), axis=0, keepdims=True)
+    n1t[...] = n1_ref[...].T
+    brt[...] = branch.T
+    dn1[...] = jnp.zeros_like(dn1)
+    low, high = halves()
+    alive = lanes((1, rows)) < SEQ
+
+    def one(h, carry):
+        weight = g_ref[h, :, 0:96, :].reshape(wide, wide)
+        from_first = nn(branch, weight[:, 640:768]).astype(BF16)
+        from_second = nn(branch, weight[:, 384:512]).astype(BF16)
+        ends = lse_ref[h]
+        slabs = [None] * 5
+        for i, (sq, sk, sv, uq, uv) in enumerate(HEADS_AT):
+            mask_q, mask_v = (high if uq else low), (high if uv else low)
+            query = qkv_ref[h, :, 128 * sq : 128 * sq + 128] * mask_q
+            key = qkv_ref[h, :, 128 * sk : 128 * sk + 128]
+            value = qkv_ref[h, :, 128 * sv : 128 * sv + 128]
+            grad = (from_first if i < 2 else from_second) * mask_v
+            scores = HEAD_DIM ** (-0.5) * nt(query, key)
+            weights = jnp.where(alive, jnp.exp(jnp.where(alive, scores - ends[:, i : i + 1], 0.0)), 0.0)
+            value_grad = tn(weights.astype(BF16), grad)
+            weight_grad = nt(grad, value)
+            inner = jnp.sum(weight_grad * weights, axis=-1, keepdims=True)
+            score = (weights * (weight_grad - inner)).astype(BF16)
+            query_grad = HEAD_DIM ** (-0.5) * nn(score, key * mask_q)
+            key_grad = HEAD_DIM ** (-0.5) * tn(score, query)
+            for at, part in ((sq, query_grad), (sk, key_grad), (sv, value_grad)):
+                slabs[at] = part if slabs[at] is None else slabs[at] + part
+        for at, slab in enumerate(slabs):
+            low_slab = slab.astype(BF16)
+            dqkv[:, 128 * at : 128 * at + 128] = low_slab
+            hb_ref[h, 0:1, 128 * at : 128 * at + 128] = jnp.sum(low_slab.astype(F32), axis=0, keepdims=True)
+        dn1[...] += nt(dqkv[...], weight[:, 0:640])
+        shape = (8, 96, 128)
+        for at in range(6):
+            if at < 5:
+                part = nn(n1t[...], dqkv[:, 128 * at : 128 * at + 128])
+                if at == 3:
+                    part += nn(brt[...], att_ref[h, :, 128:256])
+            else:
+                part = nn(brt[...], att_ref[h, :, 0:128])
+            dg_ref[h, :, :, 128 * at : 128 * at + 128] = part.astype(BF16).reshape(shape)
+        return carry
+
+    lax.fori_loop(0, 4, one, 0)
+    first_grad = dn1[...]
+    normal, inverse = normalise(x_ref[...].astype(F32))
+    scaled = first_grad * vec_ref[0:1]
+    ig_ref[...] += inverse * (
+        scaled
+        - jnp.mean(scaled, axis=-1, keepdims=True)
+        - normal * jnp.mean(scaled * normal, axis=-1, keepdims=True)
+    )
+    sm_ref[0:1] = jnp.sum(first_grad * normal, axis=0, keepdims=True)
+    sm_ref[1:2] = jnp.sum(first_grad, axis=0, keepdims=True)
+
+
+def backward_block(*operands):
+    rows, wide = operands[0].shape
+    return pl.pallas_call(
+        backward_kernel,
+        out_shape=(
+            jax.ShapeDtypeStruct((rows, wide), F32),
+            jax.ShapeDtypeStruct((rows, wide), F32),
+            jax.ShapeDtypeStruct((4, 8, 96, wide), BF16),
+            jax.ShapeDtypeStruct((4, 1, 640), F32),
+            jax.ShapeDtypeStruct((16, wide), F32),
+        ),
+        in_specs=[VM] * len(operands),
+        out_specs=(VM,) * 5,
+        scratch_shapes=[
+            pltpu.VMEM((wide, rows), BF16),
+            pltpu.VMEM((wide, rows), BF16),
+            pltpu.VMEM((rows, 640), BF16),
+            pltpu.VMEM((rows, wide), F32),
+        ],
+        compiler_params=pltpu.CompilerParams(vmem_limit_bytes=56 * MIB),
+        cost_estimate=pl.CostEstimate(flops=4 * 10**9, bytes_accessed=18 * 10**6, transcendentals=10**6),
+        name="attention_backward",
+    )(*operands)
+
+
+def staged_body(
+    inputs,
+    first_gain,
+    first_bias,
+    head_weight,
+    head_bias,
+    merge_weight,
+    merge_bias,
+    second_gain,
+    second_bias,
+    router,
+    router_noise,
+    expert_ids,
+    expert_in,
+    expert_in_bias,
+    expert_out,
+    expert_out_bias,
+    cotangent,
+):
+    tok_rows, wide = inputs.shape
+    experts = expert_in.shape[0]
+    d, h, t = lax.axis_index("dp"), lax.axis_index("heads"), lax.axis_index("tensor")
+    total_tokens = tok_rows * lax.axis_size(("dp", "heads", "tensor"))
+    extra = ROWS - tok_rows
+    chosen = jnp.sum(
+        (expert_ids[:, :, None] == jnp.arange(experts, dtype=jnp.int32)).astype(F32), axis=1
+    )
+    counts = jnp.sum(chosen, axis=0)
+    kinds = jnp.concatenate([head_weight, merge_weight.T[None]], axis=0)
+    kinds = jnp.transpose(kinds, (1, 0, 2)).reshape(96, 12, HEAD_DIM)
+    packed = jnp.concatenate([kinds[:, k] for k in CHUNKS], axis=1)
+    tiny = jnp.concatenate([head_bias.reshape(-1), expert_in_bias.reshape(-1), counts.astype(BF16)])
+    tiny = jnp.pad(tiny[None], ((0, 15), (0, wide - tiny.shape[0])))
+    shard = jnp.concatenate([packed, tiny], axis=0)
+    pieces = jnp.stack([expert_in, jnp.transpose(expert_out, (0, 2, 1))], axis=1)
+    gathered, weights = gather_weights(shard, pieces)
+    tinies = gathered[:, :, 96, :]
+    bias = tinies[:, :, 0:48].reshape(4, 8, 2, 24).transpose(2, 0, 1, 3).reshape(2, 4, 3, HEAD_DIM).astype(F32)
+    none = jnp.zeros((4, 2 * HEAD_DIM), F32)
+    head_row = jnp.concatenate(
+        [bias[0, :, 0], bias[0, :, 1], none, bias[0, :, 2], bias[1, :, 2], none, bias[1, :, 0], bias[1, :, 1]],
+        axis=1,
+    )[:, None]
+    in_bias = tinies[:, :, 48 : 48 + 96 * experts].reshape(4, 4, 2, experts, 96).transpose(3, 2, 1, 0, 4)
+    in_bias = lax.dynamic_slice(in_bias.reshape(experts, 2, 1536), (d, t, 0), (1, 1, 1536))
+    in_bias = jnp.broadcast_to(in_bias.reshape(1, 1536).astype(F32), (8, 1536))
+    count_all = jnp.sum(tinies[:, :, 48 + 96 * experts : 52 + 96 * experts].astype(F32), axis=(0, 1))
+    load_share = count_all / (2 * total_tokens)
+    vectors = jnp.stack(
+        [first_gain, first_bias, second_gain, second_bias, merge_bias] + [jnp.zeros_like(merge_bias)] * 3
+    ).astype(F32)
+    router_wide = jnp.pad(router, ((0, 0), (0, 128 - experts)))
+    noise = jnp.pad(
+        jnp.pad(router_noise, ((0, extra), (0, 0))), ((0, 0), (0, 128 - experts)), constant_values=-1e30
+    )
+    chosen_wide = jnp.pad(chosen, ((0, extra), (0, 128 - experts)))
+    spread = jnp.pad(chosen.T, ((0, 8 - experts), (0, extra)))
+    x = jnp.pad(inputs, ((0, extra), (0, 0)))
+    cot = jnp.pad(cotangent, ((0, extra), (0, 0)))
+    n1, qkv, attended, lse, residual, chances, slots, out_bias = forward_block(
+        x, gathered, head_row, vectors, router_wide, noise, spread, cot
+    )
+    received = dispatch(slots)
+    partial, weight_grads, in_bias_rows = expert_block(received, weights, in_bias)
+    own_grads = reduce_experts(weight_grads)
+    back = collect(partial)
+    load = jnp.pad((experts * load_share / total_tokens)[None], ((0, 7), (0, 128 - experts)))
+    eb = jnp.pad(expert_out_bias.astype(F32), ((0, 8 - experts), (0, 0)))
+    output, input_grad, shard_grads, head_rows, small = backward_block(
+        x,
+        gathered,
+        vectors,
+        router_wide,
+        chosen_wide,
+        spread,
+        cot,
+        load,
+        eb,
+        n1,
+        qkv,
+        attended,
+        lse,
+        residual,
+        chances,
+        out_bias,
+        back,
+    )
+    mine = (jnp.arange(experts)[:, None] == d) & (jnp.arange(2)[None, :] == t)
+    in_rows = jnp.where(mine[:, :, None], in_bias_rows[0][None, None], 0.0).reshape(16, wide)
+    head_rows = jnp.pad(head_rows.reshape(4, 640), ((0, 4), (0, wide - 640)))
+    shard_grad, sums = reduce_shards(shard_grads, jnp.concatenate([small, head_rows, in_rows], axis=0))
+    order = [CHUNKS.index(k) for k in range(12)]
+    parts = [shard_grad[:, HEAD_DIM * k : HEAD_DIM * k + HEAD_DIM] for k in order]
+    head_weight_grad = jnp.stack([jnp.concatenate(parts[3 * j : 3 * j + 3], axis=1) for j in range(3)])
+    merge_grad = jnp.concatenate(parts[9:12], axis=1).T
+    heads = lax.dynamic_slice(sums[16:20], (h, 0), (1, 640))[0]
+    biases = jnp.stack(
+        [
+            jnp.concatenate([heads[0:128], heads[256:320]]),
+            jnp.concatenate([heads[512:640], heads[320:384]]),
+        ]
+    )
+    head_bias_grad = lax.dynamic_slice(biases, (0, 24 * (2 * d + t)), (2, 24))
+    in_bias_grad = lax.dynamic_slice(
+        sums[24:40].reshape(experts, 3072), (0, 1536 * t + 96 * (4 * d + h)), (experts, 96)
+    )
+    balance_loss = experts * jnp.sum(load_share * sums[5, 0:experts] / total_tokens)
+    return (
+        output[:tok_rows],
+        balance_loss,
+        input_grad[:tok_rows],
+        sums[0],
+        sums[1],
+        head_weight_grad,
+        head_bias_grad,
+        merge_grad,
+        sums[4],
+        sums[2],
+        sums[3],
+        sums[8:12].T,
+        own_grads[:, 0].astype(F32),
+        in_bias_grad,
+        jnp.transpose(own_grads[:, 1], (0, 2, 1)).astype(F32),
+        sums[12:16],
+    )
 
 
 def layer_norm(values, factor, offset):
@@ -23,7 +869,7 @@
     )
 
 
-def body(
+def plain_body(
     inputs,
     first_gain,
     first_bias,
@@ -105,7 +951,11 @@
     expert_range = jnp.arange(experts, dtype=jnp.int32)
     chosen_pair = (expert_ids[:, :, None] == expert_range).astype(jnp.int32)
     chosen = jnp.sum(chosen_pair, axis=1)
-    before = jnp.cumsum(chosen, axis=0) - chosen
+    order = jnp.arange(tok_rows, dtype=jnp.int32)
+    earlier = (order[None, :] < order[:, None]).astype(jnp.bfloat16)
+    before = jnp.dot(
+        earlier, chosen.astype(jnp.bfloat16), preferred_element_type=jnp.float32
+    ).astype(jnp.int32)
     slot_ids = jnp.take_along_axis(before, expert_ids, axis=1)
     flat_rows = (slot_ids * experts + expert_ids).reshape(-1)
     picks = chosen_pair.astype(jnp.float32)
@@ -325,4 +1175,6 @@
         P(None, "tensor", ("dp", "heads")),
         P(),
     )
+    sizes = tuple(mesh.shape[name] for name in ("dp", "heads", "tensor"))
+    body = staged_body if sizes == (4, 4, 2) else plain_body
     return jax.shard_map(body, mesh=mesh, in_specs=in_specs, out_specs=out_specs, check_vma=False)

time: 1230 us -> 338 us (0.27)
  waiting for transfers between devices: 750 us -> 0 us
  Pallas kernels: 0 us -> 299 us
  blocking collectives: 241 us -> 0 us
  matrix products: 87.8 us -> 0 us
  local copies, waits for them, and re-layouts: 87 us -> 27.5 us
  other arithmetic: 29.6 us -> 8.32 us
  between operations: 19.5 us -> 3.16 us
    pallas_call x0 -> x8, Pallas kernels: none -> 299 us  [the longest x1 65.7 us: gather_weights(): pl.pallas_call(gather_kernel, out_shape=(jax.ShapeDtypeStruct((4, 8) + sh...]
    unnamed x17 -> x0, waiting for transfers between devices: 289 us -> none
    reduce_scatter x5 -> x0, waiting for transfers between devices: 270 us -> none  [the longest x1 199 us: body(): lax.psum_scatter(out_grad_rows, ('dp', 'heads'), scatter_dimension=0, til...]
    all_gather x6 -> x0, waiting for transfers between devices: 191 us -> none  [the longest x1 83.7 us: expert_weights(): lax.all_gather(expert_in, ('dp', 'heads'), axis=1, tiled=True)]
    all_gather x4 -> x0, blocking collectives: 109 us -> none  [the longest x1 35.3 us: body(): lax.all_gather(head_weight, ('dp', 'tensor'), axis=1, tiled=True)]
    dot_general x20 -> x0, matrix products: 86.7 us -> none  [the longest x1 12 us: body(): jnp.einsum('cef,ced->def', activated_low, pair_grad, preferred_element_ty...]
    psum x2 -> x0, blocking collectives: 79.4 us -> none  [body(): lax.psum((count_terms, chance_terms), ('dp', 'heads', 'tensor'))]
    unnamed x3 -> x0, blocking collectives: 52.7 us -> none
  transfers between devices with their start and end apart: 15 -> 0, of which waited for: 7 -> 0; matrix products, arithmetic and copies ran while one was open for 15% -> 0% of each run, Pallas kernels for 0% -> 0%
where the time goes in v1:
time: 338 us
  Pallas kernels  299 us (88%)
  local copies, waits for them, and re-layouts  27.5 us (8%)
  other arithmetic  8.32 us (2%)
    pallas_call x1, Pallas kernels, gather_weights(): pl.pallas_call(gather_kernel, out_shape=(jax.ShapeDtypeStruct((4, 8) + sh...  65.7 us
    pallas_call x1, Pallas kernels, collect(): pl.pallas_call(collect_kernel, out_shape=jax.ShapeDtypeStruct((4,) + bloc...  52.1 us
    pallas_call x1, Pallas kernels, dispatch(): pl.pallas_call(dispatch_kernel, out_shape=jax.ShapeDtypeStruct((8,) + slo...  50.1 us
    pallas_call x1, Pallas kernels, reduce_experts(): pl.pallas_call(reduce_experts_kernel, out_shape=jax.ShapeDtypeStruct((4,)...  38.8 us
    pallas_call x1, Pallas kernels, reduce_shards(): pl.pallas_call(reduce_shards_kernel, out_shape=(jax.ShapeDtypeStruct(bloc...  38 us
    pallas_call x1, Pallas kernels, expert_block(): pl.pallas_call(expert_kernel, out_shape=(jax.ShapeDtypeStruct(received.sh...  24.6 us
    pallas_call x1, Pallas kernels, backward_block(): pl.pallas_call(backward_kernel, out_shape=(jax.ShapeDtypeStruct((rows, wi...  19.6 us
    unnamed x86, local copies, waits for them, and re-layouts  18.5 us

profile of v1, /device:TPU:0, one launch (start us, length us, event | category | flops | bytes accessed | tf_op | source)
XLA Modules:
  0.0 337.5 jit_solution(9480520508475371802)
XLA Ops:
  0.7 1.2 copy.65
  1.9 0.9 pad_maximum_fusion.2
  4.6 0.7 fusion.1.a_ref
  5.3 1.1 pad_maximum_fusion.w_ref
  6.5 65.7 %gather_weights.1 = (bf16[4,8,112,768]{3,2,1,0:T(8,128)(2,1)}, bf16[2,16,48,1536]{3,2,1,0:T(8,128)(2,1)}) custom-call(bf16[112,768]{1,0:T(8,128)(2,1)} %fusion.1.a_ref, bf16[4,2,48,1536]{3,2,1,0:T(8,128)(2,1)} %pad_maximum_fusion.w_ref), custom_call_target="tpu_custom_call" | custom-call | tf_op jit(solution)/shard_map/gather_weights/pallas_call | solution.py:136
  72.2 1.1 slice.179
  74.4 9.6 %attention_forward.1 = (bf16[208,768]{1,0:T(8,128)(2,1)S(1)}, bf16[4,208,640]{2,1,0:T(8,128)(2,1)S(1)}, bf16[4,208,256]{2,1,0:T(8,128)(2,1)S(1)}, f32[4,208,128]...) custom-call(bf16[208,768]{1,0:T(8,128)(2,1)S(1)} %pad.45.x_ref, ...), custom_call_target="tpu_custom_call" | custom-call | flops 2000000000 | bytes 12000000 | tf_op jit(solution)/shard_map/attention_forward/pallas_call | solution.py:490
  84.2 1.2 copy-done.4
  85.3 1.0 copy-done.10
  86.3 0.8 copy-done.11
  87.1 0.8 copy-done.12
  87.9 0.8 copy-done.13
  88.6 0.7 copy-done.14
  90.6 50.1 %dispatch_slots.1.r_ref = bf16[8,2,128,768]{3,2,1,0:T(8,128)(2,1)} custom-call(bf16[4,2,128,768]{3,2,1,0:T(8,128)(2,1)} %copy-done.4), custom_call_target="tpu_custom_call" | custom-call | tf_op jit(solution)/shard_map/dispatch_slots/pallas_call | solution.py:191
  141.8 24.6 %expert_block.1 = (bf16[8,2,128,768]{3,2,1,0:T(8,128)(2,1)}, bf16[2,16,48,1536]{3,2,1,0:T(8,128)(2,1)}, f32[8,1536]{1,0:T(8,128)}) custom-call(bf16[8,2,128,768]{3,2,1,0:T(8,128)(2,1)} %dispatch_slots.1.r_ref, bf16[2,16,48,1536]{3,2,1,0:T(8,128)(2,1)} %get-tuple-element.45.w_ref, f32[8,1536]{1,0:T(8,128)} %broadcast_in_dim.49.b_ref), custom_call_target="tpu_custom_call" | custom-call | flops 15000000512 | bytes 16000000 | tf_op jit(solution)/shard_map/expert_block/pallas_call | solution.py:561
  166.3 1.9 copy-done.2
  168.2 52.1 %collect_rows.1.bk_ref = bf16[4,2,128,768]{3,2,1,0:T(8,128)(2,1)S(1)} custom-call(bf16[8,2,128,768]{3,2,1,0:T(8,128)(2,1)S(1)} %copy-done.2), custom_call_target="tpu_custom_call" | custom-call | tf_op jit(solution)/shard_map/collect_rows/pallas_call | solution.py:228
  220.4 1.2 copy-done.3
  222.3 0.7 pad.48.chosen_ref
  223.6 19.6 %attention_backward.1 = (f32[208,768]{1,0:T(8,128)}, f32[208,768]{1,0:T(8,128)}, bf16[4,8,96,768]{3,2,1,0:T(8,128)(2,1)}, f32[4,1,640]{2,1,0:T(1,128)}, f32[16,768]{1,0:T(8,128)}) custom-call(bf16[208,768]{1,0:T(8,128)(2,1)} %copy-done.5, bf16[4,8,112,768]{3,2,1,0:T(8,128)(2,1)} %get-tuple-element.36.g_ref, f32[8,768]{1,0:T(8,128)} %copy-done.8, ...), custom_call_target="tpu_custom_call" | custom-call | flops 4000000000 | bytes 18000000 | tf_op jit(solution)/shard_map/attention_backward/pallas_call | solution.py:707
  243.2 0.7 copy.117
  243.9 0.8 slice_reduce_fusion
  245.0 0.8 fusion.2.s_ref
  245.8 2.3 copy-done.1
  248.1 38.0 %reduce_shards.1 = (f32[96,768]{1,0:T(8,128)S(1)}, f32[40,768]{1,0:T(8,128)S(1)}) custom-call(bf16[4,8,96,768]{3,2,1,0:T(8,128)(2,1)S(1)} %copy-done.1, f32[40,768]{1,0:T(8,128)S(1)} %fusion.2.s_ref), custom_call_target="tpu_custom_call" | custom-call | tf_op jit(solution)/shard_map/reduce_shards/pallas_call | solution.py:363
  286.2 0.7 copy.89
  288.4 0.7 pad_maximum_fusion.1
  291.8 0.9 slice.189
  292.6 0.9 slice.192
  293.5 2.3 copy-done
  295.8 38.8 %reduce_experts.1 = bf16[4,2,48,1536]{3,2,1,0:T(8,128)(2,1)S(1)} custom-call(bf16[2,16,48,1536]{3,2,1,0:T(8,128)(2,1)S(1)} %copy-done), custom_call_target="tpu_custom_call" | custom-call | tf_op jit(solution)/shard_map/reduce_experts/pallas_call | solution.py:284
  334.7 1.7 convert_bitcast_fusion
  (133 shorter events, 10.1 us)
Async XLA Ops:
  0.6 3.6 %copy-start.26 = (s32[197,2]{0,1:T(2,128)S(1)}, s32[197,2]{0,1:T(2,128)}, u32[]{:S(2)}) copy-start(s32[197,2]{0,1:T(2,128)} %param.28) | copy-start | bytes 4732
  0.7 3.7 %copy-start.32 = (bf16[4,96]{1,0:T(4,128)(2,1)S(1)}, bf16[4,96]{1,0:T(4,128)(2,1)}, u32[]{:S(2)}) copy-start(bf16[4,96]{1,0:T(4,128)(2,1)} %param.30) | copy-start | bytes 2308
  0.7 3.8 %copy-start.33 = (bf16[2,24]{1,0:T(2,128)(2,1)S(1)}, bf16[2,24]{1,0:T(2,128)(2,1)}, u32[]{:S(2)}) copy-start(bf16[2,24]{1,0:T(2,128)(2,1)} %param.21) | copy-start | bytes 292
  0.7 4.7 %copy-start.20 = (bf16[4,48,1536]{2,1,0:T(8,128)(2,1)S(1)}, bf16[4,48,1536]{2,1,0:T(8,128)(2,1)}, u32[]{:S(2)}) copy-start(bf16[4,48,1536]{2,1,0:T(8,128)(2,1)} %param.29) | copy-start | bytes 1769476
  0.7 4.7 %copy-start.19 = (bf16[4,1536,48]{1,2,0:T(8,128)(2,1)S(1)}, bf16[4,1536,48]{1,2,0:T(8,128)(2,1)}, u32[]{:S(2)}) copy-start(bf16[4,1536,48]{1,2,0:T(8,128)(2,1)} %param.31) | copy-start | bytes 1769476
  6.5 67.2 %copy-start.23 = (bf16[768,4]{0,1:T(4,128)(2,1)S(1)}, bf16[768,4]{0,1:T(4,128)(2,1)}, u32[]{:S(2)}) copy-start(bf16[768,4]{0,1:T(4,128)(2,1)} %param.26) | copy-start | bytes 18436
  6.5 67.5 %copy-start.21 = (bf16[197,768]{1,0:T(8,128)(2,1)S(1)}, bf16[197,768]{1,0:T(8,128)(2,1)}, u32[]{:S(2)}) copy-start(bf16[197,768]{1,0:T(8,128)(2,1)} %param.17) | copy-start | bytes 907780
  72.2 1.9 copy-start.22
  73.3 0.8 copy-start.27
  73.3 0.8 copy-start.28
  73.3 0.8 copy-start.29
  73.3 0.8 copy-start.30
  73.3 0.9 copy-start.31
  73.3 1.0 copy-start.25
  73.7 10.4 %copy-start.9 = (f32[8,208]{1,0:T(8,128)}, f32[8,208]{1,0:T(8,128)S(1)}, u32[]{:S(2)}) copy-start(f32[8,208]{1,0:T(8,128)S(1)} %pad.49.spread_ref) | copy-start | bytes 19972
  74.0 10.1 %copy-start.7 = (bf16[768,128]{1,0:T(8,128)(2,1)}, bf16[768,128]{1,0:T(8,128)(2,1)S(1)}, u32[]{:S(2)}) copy-start(bf16[768,128]{1,0:T(8,128)(2,1)S(1)} %pad.47.router_ref) | copy-start | bytes 589828
  74.0 10.1 %copy-start.5 = (bf16[208,768]{1,0:T(8,128)(2,1)}, bf16[208,768]{1,0:T(8,128)(2,1)S(1)}, u32[]{:S(2)}) copy-start(bf16[208,768]{1,0:T(8,128)(2,1)S(1)} %pad.45.x_ref) | copy-start | bytes 958468
  74.1 10.1 %copy-start.6 = (bf16[208,768]{1,0:T(8,128)(2,1)}, bf16[208,768]{1,0:T(8,128)(2,1)S(1)}, u32[]{:S(2)}) copy-start(bf16[208,768]{1,0:T(8,128)(2,1)S(1)} %pad.50.cot_ref) | copy-start | bytes 958468
  74.3 9.9 %copy-start.8 = (f32[8,768]{1,0:T(8,128)}, f32[8,768]{1,0:T(8,128)S(1)}, u32[]{:S(2)}) copy-start(f32[8,768]{1,0:T(8,128)S(1)} %convert_element_type.72.vec_ref) | copy-start | bytes 73732
  84.1 1.2 copy-start.4
  85.3 1.0 copy-start.10
  86.3 0.8 copy-start.11
  87.1 0.8 copy-start.12
  87.9 0.8 copy-start.13
  88.6 0.7 copy-start.14
  166.3 1.9 copy-start.2
  168.2 54.8 %copy-start.24 = (bf16[4,768]{1,0:T(4,128)(2,1)S(1)}, bf16[4,768]{1,0:T(4,128)(2,1)}, u32[]{:S(2)}) copy-start(bf16[4,768]{1,0:T(4,128)(2,1)} %param.32) | copy-start | bytes 18436
  220.4 1.2 copy-start.3
  245.8 2.3 copy-start.1
  286.1 5.7 %copy-start.18 = (f32[208,768]{1,0:T(8,128)S(1)}, f32[208,768]{1,0:T(8,128)}, u32[]{:S(2)}) copy-start(f32[208,768]{1,0:T(8,128)} %get-tuple-element.47) | copy-start | bytes 1916932
  288.4 4.2 %copy-start.17 = (f32[208,768]{1,0:T(8,128)S(1)}, f32[208,768]{1,0:T(8,128)}, u32[]{:S(2)}) copy-start(f32[208,768]{1,0:T(8,128)} %get-tuple-element.53) | copy-start | bytes 1916932
  293.5 2.3 copy-start
  (2 other events, 1.3 us)

commit v2 on v0

--- a/solution.py
+++ b/solution.py
@@ -1,11 +1,1029 @@
+import functools
+
 import jax
 import jax.numpy as jnp
+import numpy as np
 from jax import lax
+from jax.experimental import pallas as pl
+from jax.experimental.pallas import tpu as pltpu
 from jax.sharding import PartitionSpec as P
 
 HEAD_DIM = 64
 SEQ = 197
 CAP = 128
+ROWS = 208
+MIB = 1 << 20
+F32 = jnp.float32
+BF16 = jnp.bfloat16
+MESH = pl.DeviceIdType.MESH
+VM = pl.BlockSpec(memory_space=pltpu.VMEM)
+SCALE = HEAD_DIM ** (-0.5)
+HEADS_AT = ((0, 1, 4, 0, 0), (0, 1, 4, 1, 1), (2, 3, 2, 0, 1))
+
+
+def nn(a, b):
+    return lax.dot_general(a, b, (((1,), (0,)), ((), ())), preferred_element_type=F32)
+
+
+def nt(a, b):
+    return lax.dot_general(a, b, (((1,), (1,)), ((), ())), preferred_element_type=F32)
+
+
+def tn(a, b):
+    return lax.dot_general(a, b, (((0,), (0,)), ((), ())), preferred_element_type=F32)
+
+
+def exact_parts(values):
+    parts = []
+    for _ in range(3):
+        part = values.astype(BF16)
+        parts.append(part)
+        values = values - part.astype(F32)
+    return parts
+
+
+def normalise(values):
+    average = jnp.mean(values, axis=-1, keepdims=True)
+    centred = values - average
+    spread = jnp.mean(centred * centred, axis=-1, keepdims=True)
+    inverse = lax.rsqrt(spread + 1e-06)
+    return centred * inverse, inverse
+
+
+def norm_back(grad, normal, inverse):
+    return inverse * (
+        grad
+        - jnp.mean(grad, axis=-1, keepdims=True)
+        - normal * jnp.mean(grad * normal, axis=-1, keepdims=True)
+    )
+
+
+def lanes(shape):
+    return lax.broadcasted_iota(jnp.int32, shape, len(shape) - 1)
+
+
+def rows_of(shape):
+    return lax.broadcasted_iota(jnp.int32, shape, 0)
+
+
+def halves():
+    low = (lanes((1, 128)) < HEAD_DIM).astype(F32)
+    return low.astype(BF16), (1 - low).astype(BF16)
+
+
+def row_of(values, at):
+    return jnp.sum(jnp.where(rows_of((values.shape[0], 1)) == at, values, 0.0), axis=0, keepdims=True)
+
+
+def as_row(column):
+    n = column.shape[0]
+    return jnp.sum(jnp.where(rows_of((n, n)) == lanes((n, n)), column, 0.0), axis=0, keepdims=True)
+
+
+def as_column(row):
+    n = row.shape[1]
+    return jnp.sum(jnp.where(rows_of((n, n)) == lanes((n, n)), row, 0.0), axis=1, keepdims=True)
+
+
+def scratch_plan(wide, units, rows):
+    shard, piece, block = (96, wide), (2, 48, units), (CAP, wide)
+    return (
+        ("a", shard, BF16),
+        ("wp", (4,) + piece, BF16),
+        ("g", (4, 4, 2) + shard, BF16),
+        ("w", (16,) + piece, BF16),
+        ("xb", piece, BF16),
+        ("p0", (16, units), BF16),
+        ("psum", (3, 16, units), BF16),
+        ("pgot", (6, 16, units), BF16),
+        ("bias", (16, units), F32),
+        ("vec", (8, wide), F32),
+        ("brow", (8, units), F32),
+        ("eb", (128, wide), BF16),
+        ("cs", (4,) + block, BF16),
+        ("gs", (4, 8, CAP), F32),
+        ("rt", (4, 2) + block, BF16),
+        ("rc", (4, 2) + block, BF16),
+        ("rg", (4, 2, 8, CAP), F32),
+        ("sel", (4, CAP, rows), BF16),
+        ("xs", (rows, wide), BF16),
+        ("cot", (rows, wide), BF16),
+        ("wide8", (128, rows), F32),
+        ("chosen", (rows, 128), F32),
+        ("spread", (8, rows), F32),
+        ("before", (8, rows), F32),
+        ("noise", (rows, 128), F32),
+        ("router", (128, wide), BF16),
+        ("n1", (rows, wide), BF16),
+        ("n2", (rows, wide), BF16),
+        ("qkv", (4, rows, 640), BF16),
+        ("att", (4, rows, 256), BF16),
+        ("lse", (4, rows, 128), F32),
+        ("res", (rows, wide), F32),
+        ("ch", (rows, 128), F32),
+        ("chp", (3, rows, 128), BF16),
+        ("hp", (4 * 8 * CAP, wide), BF16),
+        ("xt", (wide, 8 * CAP), BF16),
+        ("gt", (wide, 8 * CAP), BF16),
+        ("db", (8, units), F32),
+        ("so", (2 * CAP, wide), F32),
+        ("sb", (2 * CAP, wide), F32),
+        ("yo", (4, 2) + block, BF16),
+        ("yx", (4, 2) + block, BF16),
+        ("yg", (4, 2, 8, CAP), F32),
+        ("goto", (4,) + block, BF16),
+        ("gotx", (4,) + block, BF16),
+        ("gotg", (4, 8, CAP), F32),
+        ("bo", (4,) + block, BF16),
+        ("bx", (4,) + block, BF16),
+        ("bg", (4, 8, CAP), F32),
+        ("gotc", (8,) + piece, BF16),
+        ("gotz", (4,) + piece, BF16),
+        ("gotm", (2, wide, wide), BF16),
+        ("gotp", (3, 4) + shard, BF16),
+        ("gots", (3,) + shard, BF16),
+        ("n1t", (wide, rows), BF16),
+        ("brt", (wide, rows), BF16),
+        ("dqkv", (rows, 640), BF16),
+        ("dn1", (rows, wide), F32),
+        ("told", (rows, 128), F32),
+        ("ig", (rows, wide), F32),
+        ("e0", (16, wide), F32),
+        ("esum", (3, 16, wide), F32),
+        ("egot", (6, 16, wide), F32),
+        ("l0", (8, wide), F32),
+        ("lsum", (3, 8, wide), F32),
+        ("lgot", (6, 8, wide), F32),
+        ("d0", (3, 16, 128), F32),
+        ("dgot", (6, 16, 128), F32),
+    )
+
+
+class Buffers:
+    pass
+
+
+class Exchange:
+    def __init__(self, send_sems, recv_sems):
+        self.send_sems, self.recv_sems = send_sems, recv_sems
+        self.used = 0
+        d, h, t = lax.axis_index("dp"), lax.axis_index("heads"), lax.axis_index("tensor")
+        x, c = h // 2, h % 2
+        self.d, self.x, self.c, self.t = d, x, c, t
+        self.zh, self.zl = d // 2, d % 2
+        self.zs = (d, (d + 2) % 4, 2 * self.zh + 1 - self.zl, 2 * (1 - self.zh) + 1 - self.zl)
+        self.plane = ((1 - x, t), (x, 1 - t), (1 - x, 1 - t))
+        self.along = [self.at(z, x, c, t) for z in self.zs[1:]]
+        self.across = [self.at(d, px, c, pt) for px, pt in self.plane]
+        self.mate = self.at(d, x, 1 - c, t)
+        self.other_y = self.across[1]
+
+    @staticmethod
+    def at(d, x, c, t):
+        return (d, 2 * x + c, t)
+
+    def group(self, g):
+        return 2 * self.zh + (self.zl + g // 2) % 2, (self.x + g) % 2
+
+    def expert(self, g):
+        z, x = self.group(g)
+        return 2 * (z % 2) + x
+
+    def holder(self, g):
+        z, x = self.group(g)
+        return self.at(z, x, self.c, self.t)
+
+    def shard(self, j):
+        return 2 * ((self.x + 1 + j) % 2) + (self.c + 1 + j // 2) % 2
+
+    def slots(self, count):
+        self.used += count
+        return self.used - count
+
+    def send(self, slot, src, dst, peer):
+        pltpu.make_async_remote_copy(
+            src_ref=src,
+            dst_ref=dst,
+            send_sem=self.send_sems.at[slot],
+            recv_sem=self.recv_sems.at[slot],
+            device_id=peer,
+            device_id_type=MESH,
+        ).start()
+
+    def sent(self, slot, ref):
+        pltpu.make_async_copy(ref, ref, self.send_sems.at[slot]).wait()
+
+    def arrived(self, slot, ref):
+        pltpu.make_async_copy(ref, ref, self.recv_sems.at[slot]).wait()
+
+    def meet(self):
+        barrier = pltpu.get_barrier_semaphore()
+        peers = self.along + self.across + [self.mate, self.holder(3)]
+        for peer in peers:
+            pl.semaphore_signal(barrier, inc=1, device_id=peer, device_id_type=MESH)
+        pl.semaphore_wait(barrier, len(peers))
+
+
+class SumOverAll:
+    def __init__(self, ex, own, sums, got):
+        self.ex, self.own, self.sums, self.got = ex, own, sums, got
+        self.slot = ex.slots(6)
+
+    def start(self):
+        self.ex.send(self.slot, self.own, self.got.at[0], self.ex.mate)
+
+    def to_plane(self):
+        self.ex.arrived(self.slot, self.got.at[0])
+        self.sums[0] = self.own[...] + self.got[0]
+        for j, peer in enumerate(self.ex.across):
+            self.ex.send(self.slot + 1 + j, self.sums.at[0], self.got.at[1 + j], peer)
+
+    def to_half(self):
+        for j in range(3):
+            self.ex.arrived(self.slot + 1 + j, self.got.at[1 + j])
+        self.sums[1] = (self.sums[0] + self.got[3]) + (self.got[1] + self.got[2])
+        self.ex.send(self.slot + 4, self.sums.at[1], self.got.at[4], self.ex.along[0])
+
+    def to_pair(self):
+        self.ex.arrived(self.slot + 4, self.got.at[4])
+        self.sums[2] = self.sums[1] + self.got[4]
+        self.ex.send(self.slot + 5, self.sums.at[2], self.got.at[5], self.ex.along[1])
+
+    def result(self):
+        self.ex.arrived(self.slot + 5, self.got.at[5])
+        return self.sums[2].astype(F32) + self.got[5].astype(F32)
+
+    def done(self):
+        for k in range(6):
+            self.ex.sent(self.slot + k, self.got.at[k])
+
+
+def bias_lanes(ex):
+    chunk, lane = lanes((1, 640)) // HEAD_DIM, lanes((1, 640)) % HEAD_DIM
+    kind = jnp.where(
+        (chunk < 2) | (chunk == 4), 0, jnp.where((chunk == 5) | (chunk == 8) | (chunk == 9), 1, 2)
+    )
+    head = jnp.where((chunk == 1) | (chunk == 9), 1, jnp.where((chunk == 4) | (chunk == 5), 2, 0))
+    wanted = 24 * (2 * ex.d + ex.t) + rows_of((24, 640))
+    heads = ((HEAD_DIM * head + lane == wanted) & (kind < 2)).astype(F32).astype(BF16)
+    return heads, kind
+
+
+def hidden_lanes(ex, units):
+    wanted = 96 * (4 * ex.d + 2 * ex.x + ex.c) + rows_of((96, units))
+    return (lanes((96, units)) == wanted).astype(F32).astype(BF16)
+
+
+def pack(b, ex, inputs):
+    heads, merge, w_in, w_out = inputs
+    q, k, v = heads[0], heads[1], heads[2]
+    m = merge[...].T
+    b.a[:, 0:128] = q[:, 0:128]
+    b.a[:, 128:256] = k[:, 0:128]
+    b.a[:, 256:384] = jnp.concatenate([q[:, 128:192], v[:, 128:192]], axis=1)
+    b.a[:, 384:512] = jnp.concatenate([k[:, 128:192], m[:, 128:192]], axis=1)
+    b.a[:, 512:640] = v[:, 0:128]
+    b.a[:, 640:768] = m[:, 0:128]
+    b.wp[:, 0] = w_in[...]
+    b.wp[:, 1] = w_out[...]
+    me = 2 * ex.x + ex.c
+    b.g[3, ex.d, ex.t] = b.a[...]
+    b.w[4 * ex.d + me] = b.wp[ex.expert(0)]
+
+
+def small_operands(b, ex, ids_ref, head_bias_ref, in_bias_ref):
+    named = rows_of((4, SEQ))
+    ids = ids_ref[...]
+    b.wide8[...] = jnp.zeros_like(b.wide8)
+    b.wide8[0:4, 0:SEQ] = ((ids[0:1] == named) | (ids[1:2] == named)).astype(F32)
+    b.spread[...] = b.wide8[0:8]
+    b.chosen[...] = b.wide8[...].T
+    heads, kind = bias_lanes(ex)
+    row = nn(head_bias_ref[...], heads)
+    row = jnp.where(kind == 0, row[0:1], jnp.where(kind == 1, row[1:2], 0.0))
+    me = 2 * ex.x + ex.c
+    hidden = nn(in_bias_ref[...], hidden_lanes(ex, b.p0.shape[1]))
+    b.p0[...] = jnp.zeros_like(b.p0)
+    b.p0[0:4] = jnp.where(ex.t == 0, hidden, 0.0).astype(BF16)
+    b.p0[4:8] = jnp.where(ex.t == 1, hidden, 0.0).astype(BF16)
+    b.p0[8:12, 0:640] = jnp.where(rows_of((4, 1)) == me, row, 0.0).astype(BF16)
+    counts = jnp.sum(b.chosen[...], axis=0, keepdims=True)
+    high = jnp.floor(counts / 64)
+    middle = jnp.floor((counts - 64 * high) / 8)
+    digits = jnp.concatenate([counts - 64 * high - 8 * middle, middle, high], axis=0)
+    b.p0[12:15, 0:128] = digits.astype(BF16)
+
+
+def prepare(b, ex, x_ref, cot_ref, noise_ref, router_ref, eb_ref, vector_refs):
+    rows = b.xs.shape[0]
+    for ref, source in ((b.xs, x_ref), (b.cot, cot_ref)):
+        ref[rows - 16 : rows] = jnp.zeros((16, ref.shape[1]), BF16)
+        ref[0:SEQ] = source[...]
+    for i, ref in enumerate(vector_refs):
+        b.vec[i : i + 1] = ref[...].astype(F32).reshape(1, -1)
+    b.wide8[...] = jnp.full(b.wide8.shape, -1e30, F32)
+    b.wide8[0:4, 0:SEQ] = noise_ref[...]
+    b.noise[...] = b.wide8[...].T
+    for ref, source in ((b.router, router_ref), (b.eb, eb_ref)):
+        ref[...] = jnp.zeros_like(ref)
+        ref[0:4] = source[...]
+    values = b.xs[...].astype(F32)
+    normal, _ = normalise(values)
+    b.n1[...] = (normal * b.vec[0:1] + b.vec[1:2]).astype(BF16)
+    b.res[...] = values + b.vec[4:5]
+    earlier = (rows_of((rows, rows)) < lanes((rows, rows))).astype(F32).astype(BF16)
+    b.before[...] = nn(b.spread[...].astype(BF16), earlier)
+
+    def one(g, carry):
+        e = ex.expert(g)
+        slot = rows_of((CAP, rows)).astype(F32)
+        served = (row_of(b.before[...], e) == slot) & (row_of(b.spread[...], e) > 0.5)
+        b.sel[g] = jnp.where(served, 1.0, 0.0).astype(BF16)
+        b.cs[g] = nn(b.sel[g], b.cot[...]).astype(BF16)
+        return carry
+
+    lax.fori_loop(0, 4, one, 0)
+
+
+def attend(b, ex, h):
+    rows, wide = b.n1.shape
+    low, high = halves()
+    alive = lanes((1, rows)) < SEQ
+    weight = b.g[h].reshape(wide, wide)
+    b.qkv[h] = (nn(b.n1[...], weight[:, 0:640]) + row_of(b.bias[:, 0:640], 8 + ex.shard(h))).astype(BF16)
+    parts = []
+    ends = jnp.zeros((rows, 128), F32)
+    for i, (sq, sk, sv, uq, uv) in enumerate(HEADS_AT):
+        query = b.qkv[h, :, 128 * sq : 128 * sq + 128] * (high if uq else low)
+        key = b.qkv[h, :, 128 * sk : 128 * sk + 128]
+        value = b.qkv[h, :, 128 * sv : 128 * sv + 128] * (high if uv else low)
+        scores = jnp.where(alive, SCALE * nt(query, key), -1e30)
+        top = jnp.max(scores, axis=-1, keepdims=True)
+        raised = jnp.exp(scores - top)
+        total = jnp.sum(raised, axis=-1, keepdims=True)
+        parts.append(nn((raised / total).astype(BF16), value))
+        ends = jnp.where(lanes((1, 128)) == i, top + jnp.log(total), ends)
+    b.lse[h] = ends
+    first, second = (parts[0] + parts[1]).astype(BF16), parts[2].astype(BF16)
+    b.att[h, :, 0:128] = first
+    b.att[h, :, 128:256] = second
+    b.res[...] += nt(first, weight[:, 640:768]) + nt(second, weight[:, 384:512])
+
+
+def attend_back(b, ex, h):
+    rows, wide = b.n1.shape
+    low, high = halves()
+    alive = lanes((1, rows)) < SEQ
+    weight = b.g[h].reshape(wide, wide)
+    branch = b.ig[...].astype(BF16)
+    from_first = nn(branch, weight[:, 640:768]).astype(BF16)
+    from_second = nn(branch, weight[:, 384:512]).astype(BF16)
+    ends = b.lse[h]
+    slabs = [None] * 5
+    for i, (sq, sk, sv, uq, uv) in enumerate(HEADS_AT):
+        mask_q, mask_v = (high if uq else low), (high if uv else low)
+        query = b.qkv[h, :, 128 * sq : 128 * sq + 128] * mask_q
+        key = b.qkv[h, :, 128 * sk : 128 * sk + 128]
+        value = b.qkv[h, :, 128 * sv : 128 * sv + 128]
+        grad = (from_first if i < 2 else from_second) * mask_v
+        scores = SCALE * nt(query, key)
+        weights = jnp.where(alive, jnp.exp(jnp.where(alive, scores - ends[:, i : i + 1], 0.0)), 0.0)
+        value_grad = tn(weights.astype(BF16), grad)
+        weight_grad = nt(grad, value)
+        inner = jnp.sum(weight_grad * weights, axis=-1, keepdims=True)
+        score = (weights * (weight_grad - inner)).astype(BF16)
+        query_grad = SCALE * nn(score, key * mask_q)
+        key_grad = SCALE * tn(score, query)
+        for at, part in ((sq, query_grad), (sk, key_grad), (sv, value_grad)):
+            slabs[at] = part if slabs[at] is None else slabs[at] + part
+    for at, slab in enumerate(slabs):
+        low_slab = slab.astype(BF16)
+        b.dqkv[:, 128 * at : 128 * at + 128] = low_slab
+        b.l0[:, 128 * at : 128 * at + 128] = jnp.where(
+            rows_of((8, 1)) == 4 + ex.shard(h),
+            jnp.sum(low_slab.astype(F32), axis=0, keepdims=True),
+            b.l0[:, 128 * at : 128 * at + 128],
+        )
+    b.dn1[...] += nt(b.dqkv[...], weight[:, 0:640])
+    put = pl.ds(pl.multiple_of(wide * h, wide), wide)
+    for at in range(6):
+        if at < 5:
+            part = nn(b.n1t[...], b.dqkv[:, 128 * at : 128 * at + 128])
+            if at == 3:
+                part += nn(b.brt[...], b.att[h, :, 128:256])
+        else:
+            part = nn(b.brt[...], b.att[h, :, 0:128])
+        b.hp[put, 128 * at : 128 * at + 128] = part.astype(BF16)
+
+
+def route(b, ex):
+    normal, _ = normalise(b.res[...])
+    b.n2[...] = (normal * b.vec[2:3] + b.vec[3:4]).astype(BF16)
+    logits = nt(b.n2[...], b.router[...]) + b.noise[...]
+    raised = jnp.exp(logits - jnp.max(logits, axis=-1, keepdims=True))
+    chances = raised / jnp.sum(raised, axis=-1, keepdims=True)
+    b.ch[...] = chances
+    for i, part in enumerate(exact_parts(chances)):
+        b.chp[i] = part
+
+    def one(g, carry):
+        b.cs[g] = nn(b.sel[g], b.n2[...]).astype(BF16)
+        gates = nn(b.sel[g], b.chp[0]) + nn(b.sel[g], b.chp[1]) + nn(b.sel[g], b.chp[2])
+        gates = jnp.sum(jnp.where(lanes((1, 128)) == ex.expert(g), gates, 0.0), axis=-1, keepdims=True)
+        b.gs[g] = jnp.broadcast_to(as_row(gates), (8, CAP))
+        return carry
+
+    lax.fori_loop(0, 4, one, 0)
+
+
+def serve(b, ex, g):
+    cap, wide = b.rt.shape[2:]
+    units = b.w.shape[3]
+    step, tile = 2 * cap, wide // 2
+    x = b.rt[g].reshape(step, wide)
+    raw = b.rc[g].reshape(step, wide).astype(F32)
+    gate = jnp.concatenate([as_column(b.rg[g, 0, 0:1]), as_column(b.rg[g, 1, 0:1])], axis=0)
+    at = pl.ds(pl.multiple_of(g * step, step), step)
+    b.xt[:, at] = x.T
+    b.gt[:, at] = (gate * raw).astype(BF16).T
+    b.so[...] = jnp.zeros_like(b.so)
+    b.sb[...] = jnp.zeros_like(b.sb)
+
+    def columns(f, carry):
+        x = b.rt[g].reshape(step, wide)
+        raw = b.rc[g].reshape(step, wide).astype(F32)
+        r = (gate * raw).astype(BF16)
+        cols = pl.ds(pl.multiple_of(f * tile, tile), tile)
+        w_in = b.w[:, 0, :, cols].reshape(wide, tile)
+        w_out = b.w[:, 1, :, cols].reshape(wide, tile)
+        v = nn(x, w_in) + b.brow[0:1, cols]
+        square = v * v
+        bend = jnp.tanh(0.7978845608028654 * v * (1.0 + 0.044715 * square))
+        hidden = (0.5 * v * (1.0 + bend)).astype(BF16)
+        slope = 0.5 * (1.0 + bend) + 0.5 * v * (1.0 - bend * bend) * (
+            0.7978845608028654 * (1.0 + 3 * 0.044715 * square)
+        )
+        low = (nn(r, w_out) * slope).astype(BF16)
+        here = pl.ds(pl.multiple_of((f // 2) * 8 * cap + g * step, step), step)
+        there = pl.ds(pl.multiple_of((2 + f // 2) * 8 * cap + g * step, step), step)
+        within = pl.ds(pl.multiple_of((f % 2) * tile, tile), tile)
+        b.hp[here, within] = hidden
+        b.hp[there, within] = low
+        b.db[0:1, cols] += jnp.sum(low.astype(F32), axis=0, keepdims=True)
+        b.so[...] += nt(hidden, w_out)
+        b.sb[...] += nt(low, w_in)
+        return carry
+
+    lax.fori_loop(0, units // tile, columns, 0)
+    b.yo[g] = b.so[...].astype(BF16).reshape(2, cap, wide)
+    b.yx[g] = b.sb[...].astype(BF16).reshape(2, cap, wide)
+    told = jnp.sum(raw * b.so[...], axis=-1, keepdims=True)
+    b.yg[g, 0] = jnp.broadcast_to(as_row(told[0:cap]), (8, cap))
+    b.yg[g, 1] = jnp.broadcast_to(as_row(told[cap:step]), (8, cap))
+
+
+def weight_grads(b, half):
+    rows, slots = b.xt.shape[0] // 2, b.xt.shape[1]
+
+    def one(f, carry):
+        cols = pl.ds(pl.multiple_of(f * 256, 256), 256)
+        shape = (8, b.w.shape[2], 256)
+        take = pl.ds(pl.multiple_of(half * rows, rows), rows)
+        put = pl.ds(8 * half, 8)
+        within = pl.ds(pl.multiple_of((f % 3) * 256, 256), 256)
+        hidden = b.hp[pl.ds(pl.multiple_of((f // 3) * slots, slots), slots), within]
+        before = b.hp[pl.ds(pl.multiple_of((2 + f // 3) * slots, slots), slots), within]
+        b.w[put, 0, :, cols] = nn(b.xt[take], before).astype(BF16).reshape(shape)
+        b.w[put, 1, :, cols] = nn(b.gt[take], hidden).astype(BF16).reshape(shape)
+        return carry
+
+    lax.fori_loop(0, b.w.shape[3] // 256, one, 0)
+
+
+def back_to_branch(b, ex, total_tokens):
+    chances, chosen = b.ch[...], b.chosen[...]
+    b.told[...] = chosen * nt(b.cot[...], b.eb[...])
+    b.dn1[...] = jnp.zeros_like(b.dn1)
+
+    def one(g, carry):
+        select = b.sel[g]
+        b.dn1[...] += tn(select, b.bx[g])
+        gate = jnp.where(lanes((1, 128)) == ex.expert(g), as_column(b.bg[g, 0:1]), 0.0)
+        first, second, third = exact_parts(gate)
+        b.told[...] += tn(select, first) + tn(select, second) + tn(select, third)
+        return carry
+
+    lax.fori_loop(0, 4, one, 0)
+    chance_grad = b.told[...] + b.bias[15:16, 0:128] * (4.0 / (2.0 * total_tokens * total_tokens))
+    logit_grad = chances * (chance_grad - jnp.sum(chances * chance_grad, axis=-1, keepdims=True))
+    living = rows_of((b.n1.shape[0], 1)) < SEQ
+    logit_low = jnp.where(living, logit_grad, 0.0).astype(BF16)
+    b.e0[...] = jnp.zeros_like(b.e0)
+    b.e0[3:4, 0:128] = jnp.sum(jnp.where(living, chances, 0.0), axis=0, keepdims=True)
+    b.e0[4:8] = tn(logit_low, b.n2[...])[0:4]
+    normal, inverse = normalise(b.res[...])
+    dn2 = b.dn1[...] + nn(logit_low, b.router[...])
+    b.e0[0:1] = jnp.sum(dn2 * normal, axis=0, keepdims=True)
+    b.e0[1:2] = jnp.sum(dn2, axis=0, keepdims=True)
+    b.ig[...] = b.cot[...].astype(F32) + norm_back(dn2 * b.vec[2:3], normal, inverse)
+    branch = b.ig[...].astype(BF16)
+    b.e0[2:3] = jnp.sum(branch.astype(F32), axis=0, keepdims=True)
+    for e in range(4):
+        gate = (chances * chosen)[:, e : e + 1]
+        b.e0[8 + e : 9 + e] = jnp.sum(
+            (gate * b.cot[...].astype(F32)).astype(BF16).astype(F32), axis=0, keepdims=True
+        )
+    b.n1t[...] = b.n1[...].T
+    b.brt[...] = branch.T
+    b.dn1[...] = jnp.zeros_like(b.dn1)
+    b.l0[...] = jnp.zeros_like(b.l0)
+
+
+def combine(b, ex, out_ref):
+    gates = b.ch[...] * b.chosen[...]
+    first, second, third = exact_parts(gates)
+    b.res[...] += nn(first, b.eb[...]) + nn(second, b.eb[...]) + nn(third, b.eb[...])
+
+    def one(g, carry):
+        gates = b.ch[...] * b.chosen[...]
+        gate = jnp.sum(jnp.where(lanes((1, 128)) == ex.expert(g), gates, 0.0), axis=-1, keepdims=True)
+        b.res[...] += gate * tn(b.sel[g], b.bo[g])
+        return carry
+
+    lax.fori_loop(0, 4, one, 0)
+    out_ref[...] = b.res[0:SEQ]
+
+
+def shard_rows(h, z=0, y=0, rows=768):
+    return pl.ds(pl.multiple_of(768 * h + 192 * z + 96 * y, 96), rows)
+
+
+def add_into(ref, *others):
+    total = ref[...].astype(F32)
+    for other in others:
+        total += other[...].astype(F32)
+    ref[...] = total.astype(ref.dtype)
+
+
+def block_kernel(total_tokens, plan, *refs):
+    inputs, outputs, (send_sems, recv_sems) = refs[:17], refs[17:26], refs[26:28]
+    x_ref, cot_ref, ids_ref, noise_ref, router_ref, eb_ref = inputs[:6]
+    out_ref, ig_ref, og_ref, hw_ref, mg_ref, early_ref, late_ref, hb_ref, ib_ref = outputs
+    b = Buffers()
+    for (name, _, _), ref in zip(plan, refs[28:], strict=True):
+        setattr(b, name, ref)
+    ex = Exchange(send_sems, recv_sems)
+    d, x, c, t = ex.d, ex.x, ex.c, ex.t
+    zh, zl = ex.zh, ex.zl
+    pack(b, ex, inputs[11:15])
+    small_operands(b, ex, ids_ref, inputs[15], inputs[16])
+    tiny = SumOverAll(ex, b.p0, b.psum, b.pgot)
+    ex.meet()
+
+    fz, fp, fc = ex.slots(3), ex.slots(12), ex.slots(16)
+
+    def slot(r, j, pt):
+        return b.g.at[j, ex.zs[r], pt]
+
+    shards = ((2, 0), (3, 1), (2, 0), (3, 1))
+
+    def spread_shard(r):
+        here = slot(r, 3, t)
+        for j in range(3):
+            ex.send(fp + 4 * j + r, here, slot(r, shards[j][0], t), ex.across[j])
+        ex.send(fc + 12 + r, here, slot(r, 1, t), ex.mate)
+
+    own = slot(0, 3, t)
+    ex.send(fz, own, own, ex.along[0])
+    ex.send(fz + 1, own, own, ex.along[1])
+    spread_shard(0)
+    tiny.start()
+
+    ez, exx, ec = ex.slots(6), ex.slots(2), ex.slots(8)
+
+    def part(r, px, pc):
+        return b.w.at[4 * ex.zs[r] + 2 * px + pc]
+
+    for r in (1, 3, 2):
+        ex.send(ez + 2 * (r - 1), b.wp.at[2 * (ex.zs[r] % 2) + x], part(0, x, c), ex.along[r - 1])
+    prepare(b, ex, x_ref, cot_ref, noise_ref, router_ref, eb_ref, inputs[6:11])
+    here = slot(1, 3, t)
+    ex.arrived(fz, here)
+    ex.send(fz + 2, here, here, ex.along[1])
+    spread_shard(1)
+    for r in (2, 3):
+        ex.arrived(fz + r - 1, slot(r, 3, t))
+        spread_shard(r)
+    tiny.to_plane()
+    ct, cy = ex.slots(4), ex.slots(4)
+    for r in range(4):
+        for j, (_, pt) in enumerate(ex.plane):
+            here = slot(r, shards[j][0], pt)
+            ex.arrived(fp + 4 * j + r, here)
+            ex.send(fc + 4 * j + r, here, slot(r, shards[j][1], pt), ex.mate)
+        if r == 1:
+            tiny.to_half()
+            ex.send(exx, b.wp.at[2 * zl + 1 - x], part(0, x, c), ex.across[0])
+            ex.send(exx + 1, b.wp.at[2 * (1 - zl) + 1 - x], b.xb, ex.across[0])
+        if r == 2:
+            tiny.to_pair()
+            for g in (1, 2, 3):
+                ex.send(ct + g, b.cs.at[g], b.rc.at[g, 0], ex.holder(g))
+    ex.send(cy, b.cs.at[0], b.rc.at[0, 1], ex.other_y)
+    ex.send(ec, part(0, x, c), part(0, x, c), ex.mate)
+    b.rc[0, 0] = b.cs[0]
+    b.bias[...] = tiny.result()
+    b.bias[15:16, 0:128] = (
+        b.bias[12:13, 0:128] + 8 * b.bias[13:14, 0:128] + 64 * b.bias[14:15, 0:128]
+    )
+    b.brow[0:1] = row_of(b.bias[...], 4 * t + ex.expert(0))
+    for r in range(4):
+        for j, (_, pt) in enumerate(ex.plane + ((x, t),)):
+            ex.arrived(fc + 4 * j + r, slot(r, shards[j][1], pt))
+
+    def forward_head(h, carry):
+        attend(b, ex, h)
+
+        @pl.when(h == 0)
+        def _():
+            ex.arrived(exx, part(0, 1 - x, c))
+            ex.arrived(exx + 1, b.xb)
+            for r in (1, 3, 2):
+                source = part(0, 1 - x, c) if r == 1 else b.xb
+                ex.send(ez + 2 * (r - 1) + 1, source, part(0, 1 - x, c), ex.along[r - 1])
+            ex.send(ec + 1, part(0, 1 - x, c), part(0, 1 - x, c), ex.mate)
+
+        @pl.when(h == 1)
+        def _():
+            for g in (1, 2, 3):
+                ex.arrived(ct + g, b.rc.at[g, 0])
+                ex.send(cy + g, b.rc.at[g, 0], b.rc.at[g, 1], ex.other_y)
+
+        return carry
+
+    lax.fori_loop(0, 4, forward_head, 0)
+    for g in (1, 2, 3):
+        ex.sent(ct + g, b.cs.at[0])
+    ex.sent(cy, b.cs.at[0])
+    route(b, ex)
+
+    tt, ty, gt, gy = ex.slots(4), ex.slots(4), ex.slots(4), ex.slots(4)
+    for g in (1, 2, 3):
+        ex.send(tt + g, b.cs.at[g], b.rt.at[g, 0], ex.holder(g))
+        ex.send(gt + g, b.gs.at[g], b.rg.at[g, 0], ex.holder(g))
+    ex.send(ty, b.cs.at[0], b.rt.at[0, 1], ex.other_y)
+    ex.send(gy, b.gs.at[0], b.rg.at[0, 1], ex.other_y)
+    b.rt[0, 0] = b.cs[0]
+    b.rg[0, 0] = b.gs[0]
+    for r in (1, 2, 3):
+        here = part(r, x, c)
+        ex.arrived(ez + 2 * (r - 1), here)
+        ex.send(ec + 2 * r, here, here, ex.mate)
+    for g in (1, 2, 3):
+        ex.arrived(tt + g, b.rt.at[g, 0])
+        ex.send(ty + g, b.rt.at[g, 0], b.rt.at[g, 1], ex.other_y)
+        ex.arrived(gt + g, b.rg.at[g, 0])
+        ex.send(gy + g, b.rg.at[g, 0], b.rg.at[g, 1], ex.other_y)
+    for r in (1, 2, 3):
+        here = part(r, 1 - x, c)
+        ex.arrived(ez + 2 * (r - 1) + 1, here)
+        ex.send(ec + 2 * r + 1, here, here, ex.mate)
+    for g in range(4):
+        ex.arrived(cy + g, b.rc.at[g, 1])
+        ex.arrived(ty + g, b.rt.at[g, 1])
+        ex.arrived(gy + g, b.rg.at[g, 1])
+    for r in range(4):
+        for i, px in enumerate((x, 1 - x)):
+            ex.arrived(ec + 2 * r + i, part(r, px, 1 - c))
+    b.db[...] = jnp.zeros_like(b.db)
+
+    yx, yg, yo = ex.slots(4), ex.slots(4), ex.slots(4)
+    hx, hg, ho = ex.slots(4), ex.slots(4), ex.slots(4)
+
+    def serve_blocks(g, carry):
+        serve(b, ex, g)
+        ex.send(yx + g, b.yx.at[g, 1], b.gotx.at[g], ex.other_y)
+        ex.send(yg + g, b.yg.at[g, 1], b.gotg.at[g], ex.other_y)
+        return carry
+
+    lax.fori_loop(0, 4, serve_blocks, 0)
+
+    def give_back(g, carry):
+        ex.arrived(yx + g, b.gotx.at[g])
+        ex.arrived(yg + g, b.gotg.at[g])
+        add_into(b.yx.at[g, 0], b.gotx.at[g])
+        add_into(b.yg.at[g, 0], b.gotg.at[g])
+
+        @pl.when(g > 0)
+        def _():
+            ex.send(hx + g, b.yx.at[g, 0], b.bx.at[g], ex.holder(g))
+            ex.send(hg + g, b.yg.at[g, 0], b.bg.at[g], ex.holder(g))
+
+        return carry
+
+    lax.fori_loop(0, 3, give_back, 0)
+    b.bx[0] = b.yx[0, 0]
+    b.bg[0] = b.yg[0, 0]
+    for k in range(6):
+        ex.sent(ez + k, b.xb)
+    ex.sent(exx, b.xb)
+    ex.sent(exx + 1, b.xb)
+    for k in range(8):
+        ex.sent(ec + k, b.xb)
+
+    kc, kz, ko = ex.slots(8), ex.slots(4), ex.slots(4)
+
+    def rows_at(half, i, pc):
+        return 4 * (2 * half + i // 2) + 2 * (i % 2) + pc
+
+    def to_mate(base, half):
+        for i in range(4):
+            ex.send(kc + base + i, b.w.at[rows_at(half, i, 1 - c)], b.gotc.at[base + i], ex.mate)
+
+    weight_grads(b, 1 - zh)
+    to_mate(0, 1 - zh)
+    give_back(3, 0)
+    for g in range(4):
+        ex.send(yo + g, b.yo.at[g, 1], b.goto.at[g], ex.other_y)
+
+    def to_other_half(i, carry):
+        ex.arrived(kc + i, b.gotc.at[i])
+        at = rows_at(1 - zh, i, c)
+        add_into(b.w.at[at], b.gotc.at[i])
+        ex.send(kz + i, b.w.at[at], b.gotz.at[i], ex.along[0])
+        return carry
+
+    lax.fori_loop(0, 4, to_other_half, 0)
+    weight_grads(b, zh)
+    to_mate(4, zh)
+    for g in (1, 2, 3):
+        ex.arrived(hx + g, b.bx.at[g])
+        ex.arrived(hg + g, b.bg.at[g])
+    back_to_branch(b, ex, total_tokens)
+    sums = SumOverAll(ex, b.e0, b.esum, b.egot)
+    sums.start()
+
+    db = ex.slots(5)
+    for i in range(b.db.shape[1] // 128):
+        b.d0[0, i : i + 1] = b.db[0:1, 128 * i : 128 * i + 128]
+    ex.send(db, b.d0.at[0], b.dgot.at[0], ex.mate)
+
+    def own_half(i, carry):
+        ex.arrived(kc + 4 + i, b.gotc.at[4 + i])
+        add_into(b.w.at[rows_at(zh, i, c)], b.gotc.at[4 + i])
+        return carry
+
+    lax.fori_loop(0, 4, own_half, 0)
+
+    sm, sp, sz = ex.slots(2), ex.slots(12), ex.slots(3)
+
+    def merge_core(i):
+        ex.arrived(sm + i, b.gotm.at[i])
+
+        h = 2 + i
+        for r in (3, 2, 1, 0):
+            z = ex.zs[r]
+            add_into(b.hp.at[shard_rows(h, z, 0, 192)], b.gotm.at[i, shard_rows(0, z, 0, 192)])
+            for j in (0, 2) if i == 0 else (1,):
+                ex.send(
+                    sp + 4 * j + r,
+                    b.hp.at[shard_rows(h, z, ex.plane[j][1], 96)],
+                    b.gotp.at[j, r],
+                    ex.across[j],
+                )
+
+    def backward_head(j, carry):
+        attend_back(b, ex, j)
+
+        @pl.when(j < 2)
+        def _():
+            ex.send(sm + j, b.hp.at[shard_rows(j)], b.gotm.at[j], ex.mate)
+
+        @pl.when(j == 0)
+        def _():
+            sums.to_plane()
+            ex.arrived(db, b.dgot.at[0])
+            b.d0[1] = b.d0[0] + b.dgot[0]
+            ex.send(db + 1, b.d0.at[1], b.dgot.at[1], ex.along[0])
+
+        @pl.when(j == 1)
+        def _():
+            def one(g, carry):
+                ex.arrived(yo + g, b.goto.at[g])
+                add_into(b.yo.at[g, 0], b.goto.at[g])
+
+                @pl.when(g > 0)
+                def _():
+                    ex.send(ho + g, b.yo.at[g, 0], b.bo.at[g], ex.holder(g))
+
+                return carry
+
+            lax.fori_loop(0, 4, one, 0)
+            b.bo[0] = b.yo[0, 0]
+            sums.to_half()
+
+        @pl.when(j == 2)
+        def _():
+            merge_core(0)
+            ex.arrived(db + 1, b.dgot.at[1])
+            b.d0[2] = b.d0[1] + b.dgot[1]
+            for g in (1, 2, 3):
+                ex.send(db + 1 + g, b.d0.at[2], b.dgot.at[1 + g], ex.holder(g))
+            sums.to_pair()
+
+        return carry
+
+    lax.fori_loop(0, 4, backward_head, 0)
+    merge_core(1)
+    first_grad = b.dn1[...]
+    normal, inverse = normalise(b.xs[...].astype(F32))
+    b.l0[0:1] = jnp.sum(first_grad * normal, axis=0, keepdims=True)
+    b.l0[1:2] = jnp.sum(first_grad, axis=0, keepdims=True)
+    late = SumOverAll(ex, b.l0, b.lsum, b.lgot)
+    late.start()
+    ig_ref[...] = (b.ig[...] + norm_back(first_grad * b.vec[0:1], normal, inverse))[0:SEQ]
+    late.to_plane()
+    for g in (1, 2, 3):
+        ex.arrived(ho + g, b.bo.at[g])
+    combine(b, ex, out_ref)
+    home = 2 * x + c
+    for r in (3, 2, 1, 0):
+        for j in range(3):
+            ex.arrived(sp + 4 * j + r, b.gotp.at[j, r])
+        mine = b.hp.at[shard_rows(3, ex.zs[r], t, 96)]
+        add_into(mine, b.gotp.at[0, r], b.gotp.at[1, r], b.gotp.at[2, r])
+        if r >= 2:
+            ex.send(sz + r - 2, mine, b.gots.at[r - 2], ex.along[1])
+    late.to_half()
+    ex.arrived(sz + 1, b.gots.at[1])
+    mine = b.hp.at[shard_rows(3, ex.zs[1], t, 96)]
+    add_into(mine, b.gots.at[1])
+    ex.send(sz + 2, mine, b.gots.at[2], ex.along[0])
+    late.to_pair()
+
+    def to_owner(i, carry):
+        g = 3 - i
+        z, px = ex.group(g)
+        got = 2 * (z % 2) + px
+        ex.arrived(kz + got, b.gotz.at[got])
+        at = 4 * z + 2 * px + c
+        add_into(b.w.at[at], b.gotz.at[got])
+
+        @pl.when(g > 0)
+        def _():
+            ex.send(ko + g, b.w.at[at], og_ref.at[ex.expert(0)], ex.holder(g))
+
+        return carry
+
+    lax.fori_loop(0, 4, to_owner, 0)
+    og_ref[ex.expert(0)] = b.w[4 * d + home]
+    totals = sums.result()
+    early_ref[...] = totals
+    share = b.bias[15:16, 0:128] / (2.0 * total_tokens)
+    balance = 4.0 * jnp.sum(share * (totals[3:4, 0:128] / total_tokens), axis=-1, keepdims=True)
+    early_ref[3:4, 0:128] = jnp.broadcast_to(balance, (1, 128))
+    units = b.db.shape[1]
+    hidden_rows = jnp.zeros((8, units), F32)
+    for g in range(4):
+        if g:
+            ex.arrived(db + 1 + g, b.dgot.at[1 + g])
+        source = b.dgot.at[1 + g] if g else b.d0.at[2]
+        line = jnp.concatenate([source[i : i + 1] for i in range(units // 128)], axis=1)
+        hidden_rows = jnp.where(rows_of((8, 1)) == ex.expert(g), line, hidden_rows)
+    select = hidden_lanes(ex, units)
+    ib_ref[...] = sum(nt(part_of, select) for part_of in exact_parts(hidden_rows))[0:4]
+    late_sum = late.result()
+    late_ref[...] = late_sum
+    heads, kind = bias_lanes(ex)
+    row = row_of(late_sum, 4 + home)[:, 0:640]
+    rows = jnp.concatenate([jnp.where(kind == 0, row, 0.0), jnp.where(kind == 1, row, 0.0)], axis=0)
+    hb_ref[...] = sum(nt(part_of, heads) for part_of in exact_parts(rows))
+    ex.arrived(sz, b.gots.at[0])
+    ex.arrived(sz + 2, b.gots.at[2])
+    shard = b.hp[shard_rows(3, d, t, 96)].astype(F32) + b.gots[0].astype(F32) + b.gots[2].astype(F32)
+    for k, (whole, lane) in enumerate(((0, 256), (128, 384), (512, 320))):
+        hw_ref[k, :, 0:128] = shard[:, whole : whole + 128]
+        hw_ref[k, :, 128:192] = shard[:, lane : lane + 64]
+    mg_ref[...] = jnp.concatenate([shard[:, 640:768], shard[:, 448:512]], axis=1).T
+    for g in (1, 2, 3):
+        ex.arrived(ko + g, og_ref.at[ex.expert(g)])
+    for sum_of in (tiny, sums, late):
+        sum_of.done()
+    for k in range(3):
+        ex.sent(fz + k, b.a)
+        ex.sent(sz + k, b.a)
+    for k in range(12):
+        ex.sent(fp + k, b.a)
+        ex.sent(sp + k, b.a)
+    for k in range(16):
+        ex.sent(fc + k, b.a)
+    for g in range(4):
+        for base in (ty, yx, yo):
+            ex.sent(base + g, b.cs.at[0])
+        for base in (gy, yg):
+            ex.sent(base + g, b.gs.at[0])
+        ex.sent(kz + g, b.xb)
+    for g in (1, 2, 3):
+        for base in (cy, tt, hx, ho):
+            ex.sent(base + g, b.cs.at[0])
+        for base in (gt, hg):
+            ex.sent(base + g, b.gs.at[0])
+        ex.sent(ko + g, b.xb)
+    for k in range(8):
+        ex.sent(kc + k, b.xb)
+    for k in range(5):
+        ex.sent(db + k, b.dgot.at[0])
+    for i in range(2):
+        ex.sent(sm + i, b.gotm.at[0])
+    assert ex.used <= COPIES
+
+
+COPIES = 192
+
+
+def staged_body(
+    inputs,
+    first_gain,
+    first_bias,
+    head_weight,
+    head_bias,
+    merge_weight,
+    merge_bias,
+    second_gain,
+    second_bias,
+    router,
+    router_noise,
+    expert_ids,
+    expert_in,
+    expert_in_bias,
+    expert_out,
+    expert_out_bias,
+    cotangent,
+):
+    tok_rows, wide = inputs.shape
+    experts, _, units = expert_in.shape
+    total_tokens = tok_rows * lax.axis_size(("dp", "heads", "tensor"))
+    plan = scratch_plan(wide, units, ROWS)
+    output, input_grad, expert_grads, head_grad, merge_grad, early, late, head_bias_grad, in_bias_grad = (
+        pl.pallas_call(
+            functools.partial(block_kernel, float(total_tokens), plan),
+            out_shape=(
+                jax.ShapeDtypeStruct((tok_rows, wide), F32),
+                jax.ShapeDtypeStruct((tok_rows, wide), F32),
+                jax.ShapeDtypeStruct((experts, 2) + expert_in.shape[1:], BF16),
+                jax.ShapeDtypeStruct(head_weight.shape, F32),
+                jax.ShapeDtypeStruct(merge_weight.shape, F32),
+                jax.ShapeDtypeStruct((16, wide), F32),
+                jax.ShapeDtypeStruct((8, wide), F32),
+                jax.ShapeDtypeStruct(head_bias.shape, F32),
+                jax.ShapeDtypeStruct(expert_in_bias.shape, F32),
+            ),
+            in_specs=[VM] * 17,
+            out_specs=(VM,) * 9,
+            scratch_shapes=[pltpu.SemaphoreType.DMA((COPIES,))] * 2
+            + [pltpu.VMEM(shape, kind) for _, shape, kind in plan],
+            compiler_params=pltpu.CompilerParams(
+                collective_id=0, has_side_effects=True, vmem_limit_bytes=60 * MIB
+            ),
+            name="block",
+        )(
+            inputs,
+            cotangent,
+            expert_ids.T,
+            router_noise.T,
+            router.T,
+            expert_out_bias,
+            first_gain,
+            first_bias,
+            second_gain,
+            second_bias,
+            merge_bias,
+            head_weight,
+            merge_weight,
+            expert_in,
+            jnp.transpose(expert_out, (0, 2, 1)),
+            head_bias,
+            expert_in_bias,
+        )
+    )
+    return (
+        output,
+        early[3, 0],
+        input_grad,
+        late[0],
+        late[1],
+        head_grad,
+        head_bias_grad,
+        merge_grad,
+        early[2],
+        early[0],
+        early[1],
+        early[4:8].T,
+        expert_grads[:, 0].astype(F32),
+        in_bias_grad,
+        jnp.transpose(expert_grads[:, 1], (0, 2, 1)).astype(F32),
+        early[8:12],
+    )
 
 
 def layer_norm(values, factor, offset):
@@ -23,7 +1041,7 @@
     )
 
 
-def body(
+def plain_body(
     inputs,
     first_gain,
     first_bias,
@@ -105,7 +1123,11 @@
     expert_range = jnp.arange(experts, dtype=jnp.int32)
     chosen_pair = (expert_ids[:, :, None] == expert_range).astype(jnp.int32)
     chosen = jnp.sum(chosen_pair, axis=1)
-    before = jnp.cumsum(chosen, axis=0) - chosen
+    order = jnp.arange(tok_rows, dtype=jnp.int32)
+    earlier = (order[None, :] < order[:, None]).astype(jnp.bfloat16)
+    before = jnp.dot(
+        earlier, chosen.astype(jnp.bfloat16), preferred_element_type=jnp.float32
+    ).astype(jnp.int32)
     slot_ids = jnp.take_along_axis(before, expert_ids, axis=1)
     flat_rows = (slot_ids * experts + expert_ids).reshape(-1)
     picks = chosen_pair.astype(jnp.float32)
@@ -325,4 +1347,6 @@
         P(None, "tensor", ("dp", "heads")),
         P(),
     )
+    sizes = tuple(mesh.shape[name] for name in ("dp", "heads", "tensor"))
+    body = staged_body if sizes == (4, 4, 2) else plain_body
     return jax.shard_map(body, mesh=mesh, in_specs=in_specs, out_specs=out_specs, check_vma=False)

time: 1230 us -> 233 us (0.19)
  waiting for transfers between devices: 750 us -> 0 us
  blocking collectives: 241 us -> 0 us
  Pallas kernels: 0 us -> 219 us
  matrix products: 87.8 us -> 0 us
  local copies, waits for them, and re-layouts: 87 us -> 8.68 us
  other arithmetic: 29.6 us -> 3 us
  between operations: 19.5 us -> 0.68 us
    unnamed x17 -> x0, waiting for transfers between devices: 289 us -> none
    reduce_scatter x5 -> x0, waiting for transfers between devices: 270 us -> none  [the longest x1 199 us: body(): lax.psum_scatter(out_grad_rows, ('dp', 'heads'), scatter_dimension=0, til...]
    pallas_call x0 -> x1, Pallas kernels: none -> 219 us  [staged_body(): pl.pallas_call(functools.partial(block_kernel, float(total_tokens), plan)...]
    all_gather x6 -> x0, waiting for transfers between devices: 191 us -> none  [the longest x1 83.7 us: expert_weights(): lax.all_gather(expert_in, ('dp', 'heads'), axis=1, tiled=True)]
    all_gather x4 -> x0, blocking collectives: 109 us -> none  [the longest x1 35.3 us: body(): lax.all_gather(head_weight, ('dp', 'tensor'), axis=1, tiled=True)]
    dot_general x20 -> x0, matrix products: 86.7 us -> none  [the longest x1 12 us: body(): jnp.einsum('cef,ced->def', activated_low, pair_grad, preferred_element_ty...]
    psum x2 -> x0, blocking collectives: 79.4 us -> none  [body(): lax.psum((count_terms, chance_terms), ('dp', 'heads', 'tensor'))]
    unnamed x3 -> x0, blocking collectives: 52.7 us -> none
  transfers between devices with their start and end apart: 15 -> 0, of which waited for: 7 -> 0; matrix products, arithmetic and copies ran while one was open for 15% -> 0% of each run, Pallas kernels for 0% -> 0%
where the time goes in v2:
time: 233 us; the launch traced here: 231 us
  Pallas kernels  219 us (94%)
  local copies, waits for them, and re-layouts  8.68 us (4%)
  other arithmetic  3 us (1%)
    pallas_call x1, Pallas kernels, staged_body(): pl.pallas_call(functools.partial(block_kernel, float(total_tokens), plan)...  219 us

profile of v2, /device:TPU:0, one launch (start us, length us, event | category | flops | bytes accessed | tf_op | source)
XLA Modules:
  0.0 231.5 jit_solution(6782146084038336147)
XLA Ops:
  0.7 219.2 %block.1 = (f32[197,768]{1,0:T(8,128)}, f32[197,768]{1,0:T(8,128)}, bf16[4,2,48,1536]{3,2,1,0:T(8,128)(2,1)}, f32[3,96,192]{2,1,0:T(8,128)}, f32[192,96]{1,0:T(8...) custom-call(bf16[197,768]{1,0:T(8,128)(2,1)} %refs_0_.1, ...), custom_call_target="tpu_custom_call" | custom-call | tf_op jit(solution)/shard_map/block/pallas_call | solution.py:968
  219.8 1.2 slice.30
  221.0 1.5 slice_reduce_fusion
  222.5 1.4 fusion
  223.9 0.0 copy-start.1
  223.9 3.0 %convert_bitcast_fusion = (f32[4,1536,48]{1,2,0:T(8,128)}, f32[4,48,1536]{2,1,0:T(8,128)}) fusion(bf16[4,2,48,1536]{3,2,1,0:T(8,128)(2,1)} %get-tuple-element.32), kind=kLoop, calls=%fused_computation | loop fusion | flops 589824 | bytes 3538944 | tf_op jit(solution)/shard_map/convert_element_type | solution.py:1024
  226.9 0.0 copy-start
  226.9 0.0 copy-done.1
  226.9 0.0 copy-start.2
  226.9 0.8 copy.39
  227.7 0.5 copy-done
  228.2 0.0 copy-start.5
  228.2 0.0 copy-start.3
  228.2 0.0 copy-start.4
  228.2 0.8 copy.40
  229.0 0.0 copy-done.2
  229.0 0.7 copy.41
  229.7 0.0 copy-done.5
  229.7 0.6 copy.42
  230.3 0.0 copy-done.3
  230.3 0.6 copy.43
  230.9 0.0 copy-done.4
  230.9 0.6 copy.44
Async XLA Ops:
  223.9 3.0 %copy-start.1 = (f32[197,768]{1,0:T(8,128)S(1)}, f32[197,768]{1,0:T(8,128)}, u32[]{:S(2)}) copy-start(f32[197,768]{1,0:T(8,128)} %get-tuple-element.61) | copy-start | bytes 1815556
  226.9 1.3 copy-start
  226.9 2.1 copy-start.2
  228.2 1.5 copy-start.5
  228.2 2.1 copy-start.3
  228.2 2.8 %copy-start.4 = (f32[4,96]{1,0:T(4,128)S(1)}, f32[4,96]{1,0:T(4,128)}, u32[]{:S(2)}) copy-start(f32[4,96]{1,0:T(4,128)} %get-tuple-element.74) | copy-start | bytes 4612

commit v3 on v2

--- a/solution.py
+++ b/solution.py
@@ -126,8 +126,6 @@
         ("xt", (wide, 8 * CAP), BF16),
         ("gt", (wide, 8 * CAP), BF16),
         ("db", (8, units), F32),
-        ("so", (2 * CAP, wide), F32),
-        ("sb", (2 * CAP, wide), F32),
         ("yo", (4, 2) + block, BF16),
         ("yx", (4, 2) + block, BF16),
         ("yg", (4, 2, 8, CAP), F32),
@@ -138,7 +136,7 @@
         ("bx", (4,) + block, BF16),
         ("bg", (4, 8, CAP), F32),
         ("gotc", (8,) + piece, BF16),
-        ("gotz", (4,) + piece, BF16),
+        ("gott", (2, 4) + piece, BF16),
         ("gotm", (2, wide, wide), BF16),
         ("gotp", (3, 4) + shard, BF16),
         ("gots", (3,) + shard, BF16),
@@ -218,7 +216,8 @@
 
     def meet(self):
         barrier = pltpu.get_barrier_semaphore()
-        peers = self.along + self.across + [self.mate, self.holder(3)]
+        peers = self.along + self.across + [self.mate]
+        peers += [self.at(z, 1 - self.x, self.c, self.t) for z in self.zs[1:]]
         for peer in peers:
             pl.semaphore_signal(barrier, inc=1, device_id=peer, device_id_type=MESH)
         pl.semaphore_wait(barrier, len(peers))
@@ -439,23 +438,20 @@
 def serve(b, ex, g):
     cap, wide = b.rt.shape[2:]
     units = b.w.shape[3]
-    step, tile = 2 * cap, wide // 2
+    step = 2 * cap
     x = b.rt[g].reshape(step, wide)
     raw = b.rc[g].reshape(step, wide).astype(F32)
     gate = jnp.concatenate([as_column(b.rg[g, 0, 0:1]), as_column(b.rg[g, 1, 0:1])], axis=0)
     at = pl.ds(pl.multiple_of(g * step, step), step)
     b.xt[:, at] = x.T
     b.gt[:, at] = (gate * raw).astype(BF16).T
-    b.so[...] = jnp.zeros_like(b.so)
-    b.sb[...] = jnp.zeros_like(b.sb)
-
-    def columns(f, carry):
-        x = b.rt[g].reshape(step, wide)
-        raw = b.rc[g].reshape(step, wide).astype(F32)
+    out = jnp.zeros((step, wide), F32)
+    back = jnp.zeros((step, wide), F32)
+    for f in range(units // wide):
+        cols = slice(f * wide, f * wide + wide)
         r = (gate * raw).astype(BF16)
-        cols = pl.ds(pl.multiple_of(f * tile, tile), tile)
-        w_in = b.w[:, 0, :, cols].reshape(wide, tile)
-        w_out = b.w[:, 1, :, cols].reshape(wide, tile)
+        w_in = b.w[:, 0, :, cols].reshape(wide, wide)
+        w_out = b.w[:, 1, :, cols].reshape(wide, wide)
         v = nn(x, w_in) + b.brow[0:1, cols]
         square = v * v
         bend = jnp.tanh(0.7978845608028654 * v * (1.0 + 0.044715 * square))
@@ -464,20 +460,14 @@
             0.7978845608028654 * (1.0 + 3 * 0.044715 * square)
         )
         low = (nn(r, w_out) * slope).astype(BF16)
-        here = pl.ds(pl.multiple_of((f // 2) * 8 * cap + g * step, step), step)
-        there = pl.ds(pl.multiple_of((2 + f // 2) * 8 * cap + g * step, step), step)
-        within = pl.ds(pl.multiple_of((f % 2) * tile, tile), tile)
-        b.hp[here, within] = hidden
-        b.hp[there, within] = low
+        b.hp[pl.ds(pl.multiple_of(f * 8 * cap + g * step, step), step)] = hidden
+        b.hp[pl.ds(pl.multiple_of((2 + f) * 8 * cap + g * step, step), step)] = low
         b.db[0:1, cols] += jnp.sum(low.astype(F32), axis=0, keepdims=True)
-        b.so[...] += nt(hidden, w_out)
-        b.sb[...] += nt(low, w_in)
-        return carry
-
-    lax.fori_loop(0, units // tile, columns, 0)
-    b.yo[g] = b.so[...].astype(BF16).reshape(2, cap, wide)
-    b.yx[g] = b.sb[...].astype(BF16).reshape(2, cap, wide)
-    told = jnp.sum(raw * b.so[...], axis=-1, keepdims=True)
+        out += nt(hidden, w_out)
+        back += nt(low, w_in)
+    b.yo[g] = out.astype(BF16).reshape(2, cap, wide)
+    b.yx[g] = back.astype(BF16).reshape(2, cap, wide)
+    told = jnp.sum(raw * out, axis=-1, keepdims=True)
     b.yg[g, 0] = jnp.broadcast_to(as_row(told[0:cap]), (8, cap))
     b.yg[g, 1] = jnp.broadcast_to(as_row(told[cap:step]), (8, cap))
 
@@ -604,16 +594,20 @@
     def part(r, px, pc):
         return b.w.at[4 * ex.zs[r] + 2 * px + pc]
 
-    for r in (1, 3, 2):
+    def own_rows(r):
         ex.send(ez + 2 * (r - 1), b.wp.at[2 * (ex.zs[r] % 2) + x], part(0, x, c), ex.along[r - 1])
+
     prepare(b, ex, x_ref, cot_ref, noise_ref, router_ref, eb_ref, inputs[6:11])
     here = slot(1, 3, t)
     ex.arrived(fz, here)
     ex.send(fz + 2, here, here, ex.along[1])
+    own_rows(1)
+    own_rows(3)
     spread_shard(1)
     for r in (2, 3):
         ex.arrived(fz + r - 1, slot(r, 3, t))
         spread_shard(r)
+    own_rows(2)
     tiny.to_plane()
     ct, cy = ex.slots(4), ex.slots(4)
     for r in range(4):
@@ -621,15 +615,22 @@
             here = slot(r, shards[j][0], pt)
             ex.arrived(fp + 4 * j + r, here)
             ex.send(fc + 4 * j + r, here, slot(r, shards[j][1], pt), ex.mate)
+        if r == 0:
+            ex.send(exx, b.wp.at[2 * zl + 1 - x], part(0, x, c), ex.across[0])
+            ex.send(exx + 1, b.wp.at[2 * (1 - zl) + 1 - x], b.xb, ex.across[0])
         if r == 1:
             tiny.to_half()
-            ex.send(exx, b.wp.at[2 * zl + 1 - x], part(0, x, c), ex.across[0])
-            ex.send(exx + 1, b.wp.at[2 * (1 - zl) + 1 - x], b.xb, ex.across[0])
         if r == 2:
             tiny.to_pair()
             for g in (1, 2, 3):
                 ex.send(ct + g, b.cs.at[g], b.rc.at[g, 0], ex.holder(g))
     ex.send(cy, b.cs.at[0], b.rc.at[0, 1], ex.other_y)
+    ex.arrived(exx, part(0, 1 - x, c))
+    ex.arrived(exx + 1, b.xb)
+    for r in (1, 3, 2):
+        source = part(0, 1 - x, c) if r == 1 else b.xb
+        ex.send(ez + 2 * (r - 1) + 1, source, part(0, 1 - x, c), ex.along[r - 1])
+    ex.send(ec + 1, part(0, 1 - x, c), part(0, 1 - x, c), ex.mate)
     ex.send(ec, part(0, x, c), part(0, x, c), ex.mate)
     b.rc[0, 0] = b.cs[0]
     b.bias[...] = tiny.result()
@@ -645,15 +646,6 @@
         attend(b, ex, h)
 
         @pl.when(h == 0)
-        def _():
-            ex.arrived(exx, part(0, 1 - x, c))
-            ex.arrived(exx + 1, b.xb)
-            for r in (1, 3, 2):
-                source = part(0, 1 - x, c) if r == 1 else b.xb
-                ex.send(ez + 2 * (r - 1) + 1, source, part(0, 1 - x, c), ex.along[r - 1])
-            ex.send(ec + 1, part(0, 1 - x, c), part(0, 1 - x, c), ex.mate)
-
-        @pl.when(h == 1)
         def _():
             for g in (1, 2, 3):
                 ex.arrived(ct + g, b.rc.at[g, 0])
@@ -731,7 +723,8 @@
     for k in range(8):
         ex.sent(ec + k, b.xb)
 
-    kc, kz, ko = ex.slots(8), ex.slots(4), ex.slots(4)
+    kc, kz, kr = ex.slots(8), ex.slots(8), ex.slots(8)
+    mine = ex.expert(0)
 
     def rows_at(half, i, pc):
         return 4 * (2 * half + i // 2) + 2 * (i % 2) + pc
@@ -746,11 +739,26 @@
     for g in range(4):
         ex.send(yo + g, b.yo.at[g, 1], b.goto.at[g], ex.other_y)
 
+    def to_owner(far, i):
+        half = 1 - zh if far else zh
+        slot = 4 * (1 - far) + i
+        ex.arrived(kc + slot, b.gotc.at[slot])
+        at = rows_at(half, i, c)
+        add_into(b.w.at[at], b.gotc.at[slot])
+
+        @pl.when((far == 1) | (i != mine))
+        def _():
+            pltpu.make_async_remote_copy(
+                src_ref=b.w.at[at],
+                dst_ref=b.gott.at[far, mine],
+                send_sem=ex.send_sems.at[kz + slot],
+                recv_sem=ex.recv_sems.at[kr + 4 * far + mine],
+                device_id=ex.at(2 * half + i // 2, i % 2, c, t),
+                device_id_type=MESH,
+            ).start()
+
     def to_other_half(i, carry):
-        ex.arrived(kc + i, b.gotc.at[i])
-        at = rows_at(1 - zh, i, c)
-        add_into(b.w.at[at], b.gotc.at[i])
-        ex.send(kz + i, b.w.at[at], b.gotz.at[i], ex.along[0])
+        to_owner(1, i)
         return carry
 
     lax.fori_loop(0, 4, to_other_half, 0)
@@ -769,8 +777,7 @@
     ex.send(db, b.d0.at[0], b.dgot.at[0], ex.mate)
 
     def own_half(i, carry):
-        ex.arrived(kc + 4 + i, b.gotc.at[4 + i])
-        add_into(b.w.at[rows_at(zh, i, c)], b.gotc.at[4 + i])
+        to_owner(0, i)
         return carry
 
     lax.fori_loop(0, 4, own_half, 0)
@@ -850,37 +857,21 @@
     for r in (3, 2, 1, 0):
         for j in range(3):
             ex.arrived(sp + 4 * j + r, b.gotp.at[j, r])
-        mine = b.hp.at[shard_rows(3, ex.zs[r], t, 96)]
-        add_into(mine, b.gotp.at[0, r], b.gotp.at[1, r], b.gotp.at[2, r])
+        share = b.hp.at[shard_rows(3, ex.zs[r], t, 96)]
+        add_into(share, b.gotp.at[0, r], b.gotp.at[1, r], b.gotp.at[2, r])
         if r >= 2:
-            ex.send(sz + r - 2, mine, b.gots.at[r - 2], ex.along[1])
+            ex.send(sz + r - 2, share, b.gots.at[r - 2], ex.along[1])
     late.to_half()
     ex.arrived(sz + 1, b.gots.at[1])
-    mine = b.hp.at[shard_rows(3, ex.zs[1], t, 96)]
-    add_into(mine, b.gots.at[1])
-    ex.send(sz + 2, mine, b.gots.at[2], ex.along[0])
+    share = b.hp.at[shard_rows(3, ex.zs[1], t, 96)]
+    add_into(share, b.gots.at[1])
+    ex.send(sz + 2, share, b.gots.at[2], ex.along[0])
     late.to_pair()
 
-    def to_owner(i, carry):
-        g = 3 - i
-        z, px = ex.group(g)
-        got = 2 * (z % 2) + px
-        ex.arrived(kz + got, b.gotz.at[got])
-        at = 4 * z + 2 * px + c
-        add_into(b.w.at[at], b.gotz.at[got])
-
-        @pl.when(g > 0)
-        def _():
-            ex.send(ko + g, b.w.at[at], og_ref.at[ex.expert(0)], ex.holder(g))
-
-        return carry
-
-    lax.fori_loop(0, 4, to_owner, 0)
-    og_ref[ex.expert(0)] = b.w[4 * d + home]
     totals = sums.result()
     early_ref[...] = totals
-    share = b.bias[15:16, 0:128] / (2.0 * total_tokens)
-    balance = 4.0 * jnp.sum(share * (totals[3:4, 0:128] / total_tokens), axis=-1, keepdims=True)
+    load = b.bias[15:16, 0:128] / (2.0 * total_tokens)
+    balance = 4.0 * jnp.sum(load * (totals[3:4, 0:128] / total_tokens), axis=-1, keepdims=True)
     early_ref[3:4, 0:128] = jnp.broadcast_to(balance, (1, 128))
     units = b.db.shape[1]
     hidden_rows = jnp.zeros((8, units), F32)
@@ -905,8 +896,15 @@
         hw_ref[k, :, 0:128] = shard[:, whole : whole + 128]
         hw_ref[k, :, 128:192] = shard[:, lane : lane + 64]
     mg_ref[...] = jnp.concatenate([shard[:, 640:768], shard[:, 448:512]], axis=1).T
-    for g in (1, 2, 3):
-        ex.arrived(ko + g, og_ref.at[ex.expert(g)])
+    b.gott[0, mine] = b.w[4 * d + home]
+    for e in range(4):
+        ex.arrived(kr + 4 + e, b.gott.at[1, e])
+
+        @pl.when(e != mine)
+        def _():
+            ex.arrived(kr + e, b.gott.at[0, e])
+
+        og_ref[e] = (b.gott[0, e].astype(F32) + b.gott[1, e].astype(F32)).astype(BF16)
     for sum_of in (tiny, sums, late):
         sum_of.done()
     for k in range(3):
@@ -923,12 +921,16 @@
         for base in (gy, yg):
             ex.sent(base + g, b.gs.at[0])
         ex.sent(kz + g, b.xb)
+
+        @pl.when(g != mine)
+        def _():
+            ex.sent(kz + 4 + g, b.xb)
+
     for g in (1, 2, 3):
         for base in (cy, tt, hx, ho):
             ex.sent(base + g, b.cs.at[0])
         for base in (gt, hg):
             ex.sent(base + g, b.gs.at[0])
-        ex.sent(ko + g, b.xb)
     for k in range(8):
         ex.sent(kc + k, b.xb)
     for k in range(5):

time: 233 us -> 218 us (0.936)
  Pallas kernels: 219 us -> 205 us
    pallas_call x1, Pallas kernels: 219 us -> 205 us  [staged_body(): pl.pallas_call(functools.partial(block_kernel, float(total_tokens), plan)...]
where the time goes in v3:
time: 218 us
  Pallas kernels  205 us (94%)
  local copies, waits for them, and re-layouts  8.68 us (4%)
  other arithmetic  3 us (1%)
    pallas_call x1, Pallas kernels, staged_body(): pl.pallas_call(functools.partial(block_kernel, float(total_tokens), plan)...  205 us
    unnamed x18, local copies, waits for them, and re-layouts  4.62 us

profile of v3, /device:TPU:0, one launch (start us, length us, event | category | flops | bytes accessed | tf_op | source)
XLA Modules:
  0.0 217.7 jit_solution(1742445737506536951)
XLA Ops:
  0.7 205.3 %block.1 = (f32[197,768]{1,0:T(8,128)}, f32[197,768]{1,0:T(8,128)}, bf16[4,2,48,1536]{3,2,1,0:T(8,128)(2,1)}, f32[3,96,192]{2,1,0:T(8,128)}, f32[192,96]{1,0:T(8...) custom-call(bf16[197,768]{1,0:T(8,128)(2,1)} %refs_0_.1, ...), custom_call_target="tpu_custom_call" | custom-call | tf_op jit(solution)/shard_map/block/pallas_call | solution.py:970
  206.0 1.2 slice.30
  207.2 1.5 slice_reduce_fusion
  208.7 1.4 fusion
  210.0 0.0 copy-start.1
  210.0 3.0 %convert_bitcast_fusion = (f32[4,1536,48]{1,2,0:T(8,128)}, f32[4,48,1536]{2,1,0:T(8,128)}) fusion(bf16[4,2,48,1536]{3,2,1,0:T(8,128)(2,1)} %get-tuple-element.32), kind=kLoop, calls=%fused_computation | loop fusion | flops 589824 | bytes 3538944 | tf_op jit(solution)/shard_map/convert_element_type | solution.py:1026
  213.0 0.0 copy-start
  213.0 0.0 copy-done.1
  213.0 0.0 copy-start.2
  213.0 0.8 copy.39
  213.9 0.5 copy-done
  214.3 0.0 copy-start.5
  214.3 0.0 copy-start.3
  214.3 0.0 copy-start.4
  214.3 0.8 copy.40
  215.2 0.0 copy-done.2
  215.2 0.7 copy.41
  215.9 0.0 copy-done.5
  215.9 0.6 copy.42
  216.4 0.0 copy-done.3
  216.4 0.6 copy.43
  217.1 0.0 copy-done.4
  217.1 0.6 copy.44
Async XLA Ops:
  210.0 3.0 %copy-start.1 = (f32[197,768]{1,0:T(8,128)S(1)}, f32[197,768]{1,0:T(8,128)}, u32[]{:S(2)}) copy-start(f32[197,768]{1,0:T(8,128)} %get-tuple-element.61) | copy-start | bytes 1815556
  213.0 1.3 copy-start
  213.0 2.1 copy-start.2
  214.3 1.5 copy-start.5
  214.3 2.1 copy-start.3
  214.3 2.8 %copy-start.4 = (f32[4,96]{1,0:T(4,128)S(1)}, f32[4,96]{1,0:T(4,128)}, u32[]{:S(2)}) copy-start(f32[4,96]{1,0:T(4,128)} %get-tuple-element.74) | copy-start | bytes 4612

commit v4 on v3

--- a/solution.py
+++ b/solution.py
@@ -136,7 +136,9 @@
         ("bx", (4,) + block, BF16),
         ("bg", (4, 8, CAP), F32),
         ("gotc", (8,) + piece, BF16),
-        ("gott", (2, 4) + piece, BF16),
+        ("gotz", (2,) + piece, BF16),
+        ("gotn", (4,) + piece, BF16),
+        ("gotf", (2,) + piece, BF16),
         ("gotm", (2, wide, wide), BF16),
         ("gotp", (3, 4) + shard, BF16),
         ("gots", (3,) + shard, BF16),
@@ -198,12 +200,12 @@
         self.used += count
         return self.used - count
 
-    def send(self, slot, src, dst, peer):
+    def send(self, slot, src, dst, peer, lands=None):
         pltpu.make_async_remote_copy(
             src_ref=src,
             dst_ref=dst,
             send_sem=self.send_sems.at[slot],
-            recv_sem=self.recv_sems.at[slot],
+            recv_sem=self.recv_sems.at[slot if lands is None else lands],
             device_id=peer,
             device_id_type=MESH,
         ).start()
@@ -224,33 +226,35 @@
 
 
 class SumOverAll:
-    def __init__(self, ex, own, sums, got):
+    def __init__(self, ex, own, sums, got, z_first=False):
         self.ex, self.own, self.sums, self.got = ex, own, sums, got
         self.slot = ex.slots(6)
-
-    def start(self):
-        self.ex.send(self.slot, self.own, self.got.at[0], self.ex.mate)
-
-    def to_plane(self):
-        self.ex.arrived(self.slot, self.got.at[0])
-        self.sums[0] = self.own[...] + self.got[0]
-        for j, peer in enumerate(self.ex.across):
-            self.ex.send(self.slot + 1 + j, self.sums.at[0], self.got.at[1 + j], peer)
-
-    def to_half(self):
-        for j in range(3):
-            self.ex.arrived(self.slot + 1 + j, self.got.at[1 + j])
-        self.sums[1] = (self.sums[0] + self.got[3]) + (self.got[1] + self.got[2])
-        self.ex.send(self.slot + 4, self.sums.at[1], self.got.at[4], self.ex.along[0])
-
-    def to_pair(self):
-        self.ex.arrived(self.slot + 4, self.got.at[4])
-        self.sums[2] = self.sums[1] + self.got[4]
-        self.ex.send(self.slot + 5, self.sums.at[2], self.got.at[5], self.ex.along[1])
+        near, far = [[ex.mate], ex.across], [[ex.along[0]], [ex.along[1]]]
+        self.stages = far + near[::-1] if z_first else near + far
+        self.at, self.base = 0, 0
+
+    def received(self):
+        stage = self.stages[self.at - 1]
+        for j in range(len(stage)):
+            self.ex.arrived(self.slot + self.base + j, self.got.at[self.base + j])
+        before = self.own[...] if self.at == 1 else self.sums[self.at - 2]
+        parts = [before] + [self.got[self.base + j] for j in range(len(stage))]
+        self.base += len(stage)
+        if len(parts) == 2:
+            return parts[0].astype(F32) + parts[1].astype(F32)
+        return (parts[0].astype(F32) + parts[3].astype(F32)) + (parts[1].astype(F32) + parts[2].astype(F32))
+
+    def advance(self):
+        source = self.own
+        if self.at:
+            self.sums[self.at - 1] = self.received().astype(self.sums.dtype)
+            source = self.sums.at[self.at - 1]
+        for j, peer in enumerate(self.stages[self.at]):
+            self.ex.send(self.slot + self.base + j, source, self.got.at[self.base + j], peer)
+        self.at += 1
 
     def result(self):
-        self.ex.arrived(self.slot + 5, self.got.at[5])
-        return self.sums[2].astype(F32) + self.got[5].astype(F32)
+        return self.received()
 
     def done(self):
         for k in range(6):
@@ -587,7 +591,7 @@
     ex.send(fz, own, own, ex.along[0])
     ex.send(fz + 1, own, own, ex.along[1])
     spread_shard(0)
-    tiny.start()
+    tiny.advance()
 
     ez, exx, ec = ex.slots(6), ex.slots(2), ex.slots(8)
 
@@ -608,7 +612,7 @@
         ex.arrived(fz + r - 1, slot(r, 3, t))
         spread_shard(r)
     own_rows(2)
-    tiny.to_plane()
+    tiny.advance()
     ct, cy = ex.slots(4), ex.slots(4)
     for r in range(4):
         for j, (_, pt) in enumerate(ex.plane):
@@ -619,9 +623,9 @@
             ex.send(exx, b.wp.at[2 * zl + 1 - x], part(0, x, c), ex.across[0])
             ex.send(exx + 1, b.wp.at[2 * (1 - zl) + 1 - x], b.xb, ex.across[0])
         if r == 1:
-            tiny.to_half()
+            tiny.advance()
         if r == 2:
-            tiny.to_pair()
+            tiny.advance()
             for g in (1, 2, 3):
                 ex.send(ct + g, b.cs.at[g], b.rc.at[g, 0], ex.holder(g))
     ex.send(cy, b.cs.at[0], b.rc.at[0, 1], ex.other_y)
@@ -700,6 +704,11 @@
 
     lax.fori_loop(0, 4, serve_blocks, 0)
 
+    db = ex.slots(5)
+    for i in range(b.db.shape[1] // 128):
+        b.d0[0, i : i + 1] = b.db[0:1, 128 * i : 128 * i + 128]
+    ex.send(db, b.d0.at[0], b.dgot.at[0], ex.mate)
+
     def give_back(g, carry):
         ex.arrived(yx + g, b.gotx.at[g])
         ex.arrived(yg + g, b.gotg.at[g])
@@ -714,6 +723,9 @@
         return carry
 
     lax.fori_loop(0, 3, give_back, 0)
+    ex.arrived(db, b.dgot.at[0])
+    b.d0[1] = b.d0[0] + b.dgot[0]
+    ex.send(db + 1, b.d0.at[1], b.dgot.at[1], ex.along[0])
     b.bx[0] = b.yx[0, 0]
     b.bg[0] = b.yg[0, 0]
     for k in range(6):
@@ -739,29 +751,32 @@
     for g in range(4):
         ex.send(yo + g, b.yo.at[g, 1], b.goto.at[g], ex.other_y)
 
-    def to_owner(far, i):
-        half = 1 - zh if far else zh
-        slot = 4 * (1 - far) + i
-        ex.arrived(kc + slot, b.gotc.at[slot])
-        at = rows_at(half, i, c)
-        add_into(b.w.at[at], b.gotc.at[slot])
-
-        @pl.when((far == 1) | (i != mine))
+    def core_sum(far, i):
+        ex.arrived(kc + 4 * (1 - far) + i, b.gotc.at[4 * (1 - far) + i])
+        at = rows_at(1 - zh if far else zh, i, c)
+        add_into(b.w.at[at], b.gotc.at[4 * (1 - far) + i])
+        return b.w.at[at]
+
+    def far_rows(k, carry):
+        i = 2 * (k % 2) + jnp.where(k < 2, 1 - x, x)
+        rows = core_sum(1, i)
+
+        @pl.when(k < 2)
         def _():
-            pltpu.make_async_remote_copy(
-                src_ref=b.w.at[at],
-                dst_ref=b.gott.at[far, mine],
-                send_sem=ex.send_sems.at[kz + slot],
-                recv_sem=ex.recv_sems.at[kr + 4 * far + mine],
-                device_id=ex.at(2 * half + i // 2, i % 2, c, t),
-                device_id_type=MESH,
-            ).start()
-
-    def to_other_half(i, carry):
-        to_owner(1, i)
+            ex.send(kz + k, rows, b.gotz.at[k], ex.along[0], kr + k)
+
+        @pl.when(k >= 2)
+        def _():
+            owner = ex.at(2 * (1 - zh) + k % 2, x, c, t)
+            ex.send(kz + k, rows, b.gotf.at[ex.zl], owner, kr + 2 + ex.zl)
+
         return carry
 
-    lax.fori_loop(0, 4, to_other_half, 0)
+    ex.arrived(db + 1, b.dgot.at[1])
+    b.d0[2] = b.d0[1] + b.dgot[1]
+    for g in (1, 2, 3):
+        ex.send(db + 1 + g, b.d0.at[2], b.dgot.at[1 + g], ex.holder(g))
+    lax.fori_loop(0, 4, far_rows, 0)
     weight_grads(b, zh)
     to_mate(4, zh)
     for g in (1, 2, 3):
@@ -769,18 +784,22 @@
         ex.arrived(hg + g, b.bg.at[g])
     back_to_branch(b, ex, total_tokens)
     sums = SumOverAll(ex, b.e0, b.esum, b.egot)
-    sums.start()
-
-    db = ex.slots(5)
-    for i in range(b.db.shape[1] // 128):
-        b.d0[0, i : i + 1] = b.db[0:1, 128 * i : 128 * i + 128]
-    ex.send(db, b.d0.at[0], b.dgot.at[0], ex.mate)
-
-    def own_half(i, carry):
-        to_owner(0, i)
+    sums.advance()
+
+    def near_sum(i, carry):
+        core_sum(0, i)
         return carry
 
-    lax.fori_loop(0, 4, own_half, 0)
+    lax.fori_loop(0, 4, near_sum, 0)
+    beside = b.w.at[4 * ex.zs[2] + 2 * x + c]
+    ex.send(kz + 4, beside, b.gotn.at[mine], ex.along[1], kr + 4 + mine)
+
+    def near_rows():
+        for k in range(2):
+            ex.arrived(kr + k, b.gotz.at[k])
+            at = 4 * (2 * zh + k) + 2 * (1 - x) + c
+            add_into(b.w.at[at], b.gotz.at[k])
+            ex.send(kz + 5 + k, b.w.at[at], b.gotn.at[mine], ex.at(2 * zh + k, 1 - x, c, t), kr + 4 + mine)
 
     sm, sp, sz = ex.slots(2), ex.slots(12), ex.slots(3)
 
@@ -806,13 +825,6 @@
         def _():
             ex.send(sm + j, b.hp.at[shard_rows(j)], b.gotm.at[j], ex.mate)
 
-        @pl.when(j == 0)
-        def _():
-            sums.to_plane()
-            ex.arrived(db, b.dgot.at[0])
-            b.d0[1] = b.d0[0] + b.dgot[0]
-            ex.send(db + 1, b.d0.at[1], b.dgot.at[1], ex.along[0])
-
         @pl.when(j == 1)
         def _():
             def one(g, carry):
@@ -827,29 +839,26 @@
 
             lax.fori_loop(0, 4, one, 0)
             b.bo[0] = b.yo[0, 0]
-            sums.to_half()
 
         @pl.when(j == 2)
         def _():
             merge_core(0)
-            ex.arrived(db + 1, b.dgot.at[1])
-            b.d0[2] = b.d0[1] + b.dgot[1]
-            for g in (1, 2, 3):
-                ex.send(db + 1 + g, b.d0.at[2], b.dgot.at[1 + g], ex.holder(g))
-            sums.to_pair()
 
         return carry
 
     lax.fori_loop(0, 4, backward_head, 0)
     merge_core(1)
+    near_rows()
+    sums.advance()
     first_grad = b.dn1[...]
     normal, inverse = normalise(b.xs[...].astype(F32))
     b.l0[0:1] = jnp.sum(first_grad * normal, axis=0, keepdims=True)
     b.l0[1:2] = jnp.sum(first_grad, axis=0, keepdims=True)
     late = SumOverAll(ex, b.l0, b.lsum, b.lgot)
-    late.start()
+    late.advance()
     ig_ref[...] = (b.ig[...] + norm_back(first_grad * b.vec[0:1], normal, inverse))[0:SEQ]
-    late.to_plane()
+    sums.advance()
+    late.advance()
     for g in (1, 2, 3):
         ex.arrived(ho + g, b.bo.at[g])
     combine(b, ex, out_ref)
@@ -861,12 +870,13 @@
         add_into(share, b.gotp.at[0, r], b.gotp.at[1, r], b.gotp.at[2, r])
         if r >= 2:
             ex.send(sz + r - 2, share, b.gots.at[r - 2], ex.along[1])
-    late.to_half()
+    sums.advance()
+    late.advance()
     ex.arrived(sz + 1, b.gots.at[1])
     share = b.hp.at[shard_rows(3, ex.zs[1], t, 96)]
     add_into(share, b.gots.at[1])
     ex.send(sz + 2, share, b.gots.at[2], ex.along[0])
-    late.to_pair()
+    late.advance()
 
     totals = sums.result()
     early_ref[...] = totals
@@ -896,15 +906,17 @@
         hw_ref[k, :, 0:128] = shard[:, whole : whole + 128]
         hw_ref[k, :, 128:192] = shard[:, lane : lane + 64]
     mg_ref[...] = jnp.concatenate([shard[:, 640:768], shard[:, 448:512]], axis=1).T
-    b.gott[0, mine] = b.w[4 * d + home]
+    b.gotn[mine] = b.w[4 * d + home]
+    for k in range(2):
+        ex.arrived(kr + 2 + k, b.gotf.at[k])
     for e in range(4):
-        ex.arrived(kr + 4 + e, b.gott.at[1, e])
 
         @pl.when(e != mine)
         def _():
-            ex.arrived(kr + e, b.gott.at[0, e])
-
-        og_ref[e] = (b.gott[0, e].astype(F32) + b.gott[1, e].astype(F32)).astype(BF16)
+            ex.arrived(kr + 4 + e, b.gotn.at[e])
+
+        far = jnp.where(x == e % 2, b.gotf[e // 2].astype(F32), 0.0)
+        og_ref[e] = (b.gotn[e].astype(F32) + far).astype(BF16)
     for sum_of in (tiny, sums, late):
         sum_of.done()
     for k in range(3):
@@ -920,12 +932,6 @@
             ex.sent(base + g, b.cs.at[0])
         for base in (gy, yg):
             ex.sent(base + g, b.gs.at[0])
-        ex.sent(kz + g, b.xb)
-
-        @pl.when(g != mine)
-        def _():
-            ex.sent(kz + 4 + g, b.xb)
-
     for g in (1, 2, 3):
         for base in (cy, tt, hx, ho):
             ex.sent(base + g, b.cs.at[0])
@@ -933,6 +939,8 @@
             ex.sent(base + g, b.gs.at[0])
     for k in range(8):
         ex.sent(kc + k, b.xb)
+    for k in range(7):
+        ex.sent(kz + k, b.xb)
     for k in range(5):
         ex.sent(db + k, b.dgot.at[0])
     for i in range(2):

time: 218 us -> 211 us (0.968)
  Pallas kernels: 205 us -> 199 us
    pallas_call x1, Pallas kernels: 205 us -> 199 us  [staged_body(): pl.pallas_call(functools.partial(block_kernel, float(total_tokens), plan)...]
where the time goes in v4:
time: 211 us
  Pallas kernels  199 us (94%)
  local copies, waits for them, and re-layouts  8.68 us (4%)
  other arithmetic  3 us (1%)
    pallas_call x1, Pallas kernels, staged_body(): pl.pallas_call(functools.partial(block_kernel, float(total_tokens), plan)...  199 us
    unnamed x18, local copies, waits for them, and re-layouts  4.62 us

profile of v4, /device:TPU:0, one launch (start us, length us, event | category | flops | bytes accessed | tf_op | source)
XLA Modules:
  0.0 211.1 jit_solution(15118945170931017980)
XLA Ops:
  0.7 198.7 %block.1 = (f32[197,768]{1,0:T(8,128)}, f32[197,768]{1,0:T(8,128)}, bf16[4,2,48,1536]{3,2,1,0:T(8,128)(2,1)}, f32[3,96,192]{2,1,0:T(8,128)}, f32[192,96]{1,0:T(8...) custom-call(bf16[197,768]{1,0:T(8,128)(2,1)} %refs_0_.1, ...), custom_call_target="tpu_custom_call" | custom-call | tf_op jit(solution)/shard_map/block/pallas_call | solution.py:978
  199.4 1.2 slice.30
  200.6 1.5 slice_reduce_fusion
  202.1 1.4 fusion
  203.4 0.0 copy-start.1
  203.4 3.0 %convert_bitcast_fusion = (f32[4,1536,48]{1,2,0:T(8,128)}, f32[4,48,1536]{2,1,0:T(8,128)}) fusion(bf16[4,2,48,1536]{3,2,1,0:T(8,128)(2,1)} %get-tuple-element.32), kind=kLoop, calls=%fused_computation | loop fusion | flops 589824 | bytes 3538944 | tf_op jit(solution)/shard_map/convert_element_type | solution.py:1034
  206.4 0.0 copy-start
  206.4 0.0 copy-done.1
  206.4 0.0 copy-start.2
  206.4 0.8 copy.39
  207.3 0.5 copy-done
  207.7 0.0 copy-start.5
  207.7 0.0 copy-start.3
  207.7 0.0 copy-start.4
  207.7 0.8 copy.40
  208.6 0.0 copy-done.2
  208.6 0.7 copy.41
  209.3 0.0 copy-done.5
  209.3 0.6 copy.42
  209.8 0.0 copy-done.3
  209.8 0.6 copy.43
  210.5 0.0 copy-done.4
  210.5 0.6 copy.44
Async XLA Ops:
  203.4 3.0 %copy-start.1 = (f32[197,768]{1,0:T(8,128)S(1)}, f32[197,768]{1,0:T(8,128)}, u32[]{:S(2)}) copy-start(f32[197,768]{1,0:T(8,128)} %get-tuple-element.61) | copy-start | bytes 1815556
  206.4 1.3 copy-start
  206.4 2.1 %copy-start.2 = (f32[3,96,192]{2,1,0:T(8,128)S(1)}, f32[3,96,192]{2,1,0:T(8,128)}, u32[]{:S(2)}) copy-start(f32[3,96,192]{2,1,0:T(8,128)} %get-tuple-element.66) | copy-start | bytes 663556
  207.7 1.5 copy-start.5
  207.7 2.1 %copy-start.3 = (f32[192,96]{1,0:T(8,128)S(1)}, f32[192,96]{1,0:T(8,128)}, u32[]{:S(2)}) copy-start(f32[192,96]{1,0:T(8,128)} %get-tuple-element.68) | copy-start | bytes 221188
  207.7 2.8 %copy-start.4 = (f32[4,96]{1,0:T(4,128)S(1)}, f32[4,96]{1,0:T(4,128)}, u32[]{:S(2)}) copy-start(f32[4,96]{1,0:T(4,128)} %get-tuple-element.74) | copy-start | bytes 4612

commit v5 on v4

--- a/solution.py
+++ b/solution.py
@@ -848,7 +848,6 @@
 
     lax.fori_loop(0, 4, backward_head, 0)
     merge_core(1)
-    near_rows()
     sums.advance()
     first_grad = b.dn1[...]
     normal, inverse = normalise(b.xs[...].astype(F32))
@@ -859,9 +858,6 @@
     ig_ref[...] = (b.ig[...] + norm_back(first_grad * b.vec[0:1], normal, inverse))[0:SEQ]
     sums.advance()
     late.advance()
-    for g in (1, 2, 3):
-        ex.arrived(ho + g, b.bo.at[g])
-    combine(b, ex, out_ref)
     home = 2 * x + c
     for r in (3, 2, 1, 0):
         for j in range(3):
@@ -870,12 +866,16 @@
         add_into(share, b.gotp.at[0, r], b.gotp.at[1, r], b.gotp.at[2, r])
         if r >= 2:
             ex.send(sz + r - 2, share, b.gots.at[r - 2], ex.along[1])
+    near_rows()
     sums.advance()
     late.advance()
     ex.arrived(sz + 1, b.gots.at[1])
     share = b.hp.at[shard_rows(3, ex.zs[1], t, 96)]
     add_into(share, b.gots.at[1])
     ex.send(sz + 2, share, b.gots.at[2], ex.along[0])
+    for g in (1, 2, 3):
+        ex.arrived(ho + g, b.bo.at[g])
+    combine(b, ex, out_ref)
     late.advance()
 
     totals = sums.result()

time: 211 us -> 204 us (0.967)
  Pallas kernels: 199 us -> 191 us
    pallas_call x1, Pallas kernels: 199 us -> 191 us  [staged_body(): pl.pallas_call(functools.partial(block_kernel, float(total_tokens), plan)...]
where the time goes in v5:
time: 204 us
  Pallas kernels  191 us (94%)
  local copies, waits for them, and re-layouts  8.68 us (4%)
  other arithmetic  3 us (1%)
    pallas_call x1, Pallas kernels, staged_body(): pl.pallas_call(functools.partial(block_kernel, float(total_tokens), plan)...  191 us
    unnamed x18, local copies, waits for them, and re-layouts  4.62 us

profile of v5, /device:TPU:0, one launch (start us, length us, event | category | flops | bytes accessed | tf_op | source)
XLA Modules:
  0.0 203.7 jit_solution(13063570073289443626)
XLA Ops:
  0.7 191.4 %block.1 = (f32[197,768]{1,0:T(8,128)}, f32[197,768]{1,0:T(8,128)}, bf16[4,2,48,1536]{3,2,1,0:T(8,128)(2,1)}, f32[3,96,192]{2,1,0:T(8,128)}, f32[192,96]{1,0:T(8...) custom-call(bf16[197,768]{1,0:T(8,128)(2,1)} %refs_0_.1, ...), custom_call_target="tpu_custom_call" | custom-call | tf_op jit(solution)/shard_map/block/pallas_call | solution.py:978
  192.0 1.2 slice.30
  193.2 1.5 slice_reduce_fusion
  194.7 1.4 fusion
  196.1 0.0 copy-start.1
  196.1 3.0 %convert_bitcast_fusion = (f32[4,1536,48]{1,2,0:T(8,128)}, f32[4,48,1536]{2,1,0:T(8,128)}) fusion(bf16[4,2,48,1536]{3,2,1,0:T(8,128)(2,1)} %get-tuple-element.32), kind=kLoop, calls=%fused_computation | loop fusion | flops 589824 | bytes 3538944 | tf_op jit(solution)/shard_map/convert_element_type | solution.py:1034
  199.1 0.0 copy-start
  199.1 0.0 copy-done.1
  199.1 0.0 copy-start.2
  199.1 0.8 copy.39
  199.9 0.5 copy-done
  200.4 0.0 copy-start.5
  200.4 0.0 copy-start.3
  200.4 0.0 copy-start.4
  200.4 0.8 copy.40
  201.2 0.0 copy-done.2
  201.2 0.7 copy.41
  201.9 0.0 copy-done.5
  201.9 0.6 copy.42
  202.5 0.0 copy-done.3
  202.5 0.6 copy.43
  203.1 0.0 copy-done.4
  203.1 0.6 copy.44
Async XLA Ops:
  196.1 3.0 %copy-start.1 = (f32[197,768]{1,0:T(8,128)S(1)}, f32[197,768]{1,0:T(8,128)}, u32[]{:S(2)}) copy-start(f32[197,768]{1,0:T(8,128)} %get-tuple-element.61) | copy-start | bytes 1815556
  199.1 1.3 copy-start
  199.1 2.1 %copy-start.2 = (f32[3,96,192]{2,1,0:T(8,128)S(1)}, f32[3,96,192]{2,1,0:T(8,128)}, u32[]{:S(2)}) copy-start(f32[3,96,192]{2,1,0:T(8,128)} %get-tuple-element.66) | copy-start | bytes 663556
  200.4 1.5 copy-start.5
  200.4 2.1 %copy-start.3 = (f32[192,96]{1,0:T(8,128)S(1)}, f32[192,96]{1,0:T(8,128)}, u32[]{:S(2)}) copy-start(f32[192,96]{1,0:T(8,128)} %get-tuple-element.68) | copy-start | bytes 221188
  200.4 2.8 %copy-start.4 = (f32[4,96]{1,0:T(4,128)S(1)}, f32[4,96]{1,0:T(4,128)}, u32[]{:S(2)}) copy-start(f32[4,96]{1,0:T(4,128)} %get-tuple-element.74) | copy-start | bytes 4612
